TPU v7x, 32 devices: a whole 2x2x4 slice. The times are simulated.
32 devices in a mesh: grp: 2 (over y), seq: 4 (over z), batch: 4 (over x, core).
Axes of the slice: x: 2, y: 2, z: 4, core: 2. Of those that a mesh axis runs over, the one named last changes fastest.
Arguments:
- head_split_gradient: bfloat16 [8, 768, 2048], P(('grp', 'batch'), 'seq'), parts along dimension 0, may hold values from -6 to 6
- first_layer_input: bfloat16 [8, 768, 2048], P(('grp', 'batch'), None, 'seq'), parts along dimension 0, may hold values from -40 to 40
- second_layer_input: bfloat16 [8, 768, 2048], P(('grp', 'batch'), None, 'seq'), parts along dimension 0, may hold values from -40 to 40
- first_layer_weight: bfloat16 [3, 768, 768], replicated, may hold values from -0.125 to 0.125
- second_layer_weight: bfloat16 [3, 768, 768], replicated, may hold values from -0.125 to 0.125
- first_norm_gain: float32 [768], replicated, may hold values from 0.1 to 1.9
- second_norm_gain: float32 [768], replicated, may hold values from 0.1 to 1.9
Outputs:
- input_gradient_total: bfloat16 [8, 768, 2048], P(('grp', 'batch'), None, 'seq'), parts along dimension 0
- first_weight_gradient: float32 [4608, 768], P(('grp', 'seq')), parts along dimension 0
There are 2 independent parts, one for each index of `grp`. A program takes and returns all parts, laid end to end along the dimension named above; an argument that names none is the same for every part. Nothing has to cross between parts.
All inputs are finite; a program needn't handle non-finite values.
Results may differ from a plain program's by a relative error of at most 0.005.
Values may be sent and summed in bfloat16 or wider, within the bound.
No kernel may reach another device: no remote copies, remote signals or barrier semaphores. Data moves between devices by JAX's collectives and lax.ppermute only.
A program may use at most 64 MiB of HBM per device.

v0:
```python
import math

import jax
import jax.numpy as jnp
from jax import lax
from jax.sharding import PartitionSpec as P

DILATION_FIRST = 512
DILATION_SECOND = 1024


EPS = 1e-06
SLOPE = math.sqrt(2.0 / math.pi)
CUBIC = 0.044715


def shifted(value, axis, steps):
    count = lax.axis_size(axis)
    initial, last = (max(0, -steps), min(count, count - steps))
    return lax.ppermute(value, axis, [(source, source + steps) for source in range(initial, last)])


def gelu_slope(normed):
    inner = jnp.tanh(SLOPE * (normed + CUBIC * normed * normed * normed))
    return 0.5 * (1.0 + inner) + 0.5 * normed * (1.0 - inner * inner) * SLOPE * (
        1.0 + 3.0 * CUBIC * normed * normed
    )


def prepare(inputs, gain_vec):
    xfloat = inputs.astype(jnp.float32)
    meansq = jnp.mean(xfloat * xfloat, axis=1, keepdims=True)
    scale = lax.rsqrt(meansq + EPS)
    normed = xfloat * scale * gain_vec[None, :, None]
    gelu_out = jax.nn.gelu(normed, approximate=True).astype(jnp.bfloat16)
    return (xfloat, scale, normed, gelu_out)


def border_rows(grad_out, shard_span):
    lower_grad = shifted(grad_out, "seq", shard_span)
    upper_grad = shifted(grad_out, "seq", -shard_span)
    return (lower_grad, upper_grad)


def input_grad(xfloat, scale, normed, gain_vec, weight, grad_out, grad_upper, grad_lower):
    dgelu = jnp.einsum("co,sop->scp", weight[0], grad_upper, preferred_element_type=jnp.float32)
    dgelu = dgelu + jnp.einsum(
        "co,sop->scp", weight[1], grad_out, preferred_element_type=jnp.float32
    )
    dgelu = dgelu + jnp.einsum(
        "co,sop->scp", weight[2], grad_lower, preferred_element_type=jnp.float32
    )
    dnorm = dgelu * gelu_slope(normed) * gain_vec[None, :, None]
    inner = jnp.mean(dnorm * xfloat, axis=1, keepdims=True)
    dinput = scale * dnorm - xfloat * scale * scale * scale * inner
    return (grad_out.astype(jnp.float32) + dinput).astype(jnp.bfloat16)


def local_terms(gelu_out, grad_upper, grad_out, grad_lower, scale_factor):
    pieces = [
        jnp.einsum("scp,sop->co", gelu_out, tapped, preferred_element_type=jnp.float32)
        for tapped in (grad_upper, grad_out, grad_lower)
    ]
    return jnp.concatenate(pieces, axis=0) * scale_factor


def on_device(
    head_split_gradient,
    first_layer_input,
    second_layer_input,
    first_layer_weight,
    second_layer_weight,
    first_norm_gain,
    second_norm_gain,
):
    second_layer_gradient = lax.all_to_all(
        head_split_gradient, "seq", split_axis=2, concat_axis=1, tiled=True
    )
    border_width = first_layer_input.shape[2]
    scale_factor = 1.0 / math.sqrt(
        first_layer_input.shape[0] * lax.axis_size("batch") * border_width * lax.axis_size("seq")
    )
    xfloat_two, scale_two, normed_two, gelu_two = prepare(second_layer_input, second_norm_gain)
    second_lower_border, second_upper_border = border_rows(
        second_layer_gradient, DILATION_SECOND // border_width
    )
    middle_gradient = input_grad(
        xfloat_two,
        scale_two,
        normed_two,
        second_norm_gain,
        second_layer_weight,
        second_layer_gradient,
        second_upper_border,
        second_lower_border,
    )
    xfloat_one, scale_one, normed_one, gelu_one = prepare(first_layer_input, first_norm_gain)
    first_lower_border, first_upper_border = border_rows(
        middle_gradient, DILATION_FIRST // border_width
    )
    input_gradient_total = input_grad(
        xfloat_one,
        scale_one,
        normed_one,
        first_norm_gain,
        first_layer_weight,
        middle_gradient,
        first_upper_border,
        first_lower_border,
    )
    terms_one = local_terms(
        gelu_one, first_upper_border, middle_gradient, first_lower_border, scale_factor
    )
    partial_rows = lax.psum_scatter(terms_one, "seq", scatter_dimension=0, tiled=True)
    first_weight_gradient = lax.psum(partial_rows, "batch")
    return (input_gradient_total, first_weight_gradient)


def solution(mesh):
    in_specs = (
        P(("grp", "batch"), "seq", None),
        P(("grp", "batch"), None, "seq"),
        P(("grp", "batch"), None, "seq"),
        P(),
        P(),
        P(),
        P(),
    )
    out_specs = (P(("grp", "batch"), None, "seq"), P(("grp", "seq"), None))
    return jax.shard_map(
        on_device, mesh=mesh, in_specs=in_specs, out_specs=out_specs, check_vma=False
    )
```

profile of v0, /device:TPU:0, one launch (start us, length us, event | category | flops | bytes accessed | tf_op | source)
XLA Modules:
  0.0 307.9 jit_solution(13687782460259518762)
XLA Ops:
  7.2 4.5 %copy.23 = bf16[1,192,2048]{1,0,2:T(2,128)(2,1)S(1)} copy(bf16[1,192,2048]{2,1,0:T(8,128)(2,1)} %param.7) | data formatting | bytes 1572864 | tf_op args[0]
  12.3 11.6 %reduce.4 = bf16[2048,192]{1,0:T(8,128)(2,1)S(1)} reduce(bf16[2048,1,192]{2,1,0:T(2,128)(2,1)S(1)} %bitcast.70, bf16[]{:T(256)} %broadcast.102), dimensions={1}, to_apply=%bitcast.59.reduce_sub_computation | reduce | bytes 1572866
  23.9 1.4 reshape.110
  25.3 26.3 %all_to_all.18 = bf16[4,2,49152]{2,1,0:T(2,128)(2,1)S(1)} all-to-all(bf16[4,2,49152]{2,1,0:T(2,128)(2,1)S(1)} %reshape.110), channel_id=1, replica_groups=mesh['grp'=2,'seq'=4,'batch'=4] {'seq'}, dimensions={0} | all-to-all | bytes 1572864 | tf_op jit(solution)/shard_map/all_to_all | solution.py:76
  51.5 1.4 reshape.111
  52.9 1.2 copy.24
  54.9 1.4 collective-permute-start
  56.8 6.4 %collective-permute-start.1 = (bf16[1,768,512]{2,1,0:T(8,128)(2,1)S(1)}, bf16[1,768,512]{2,1,0:T(8,128)(2,1)S(1)}, u32[]{:S(2)}, u32[]{:S(2)}) collective-permute-start(bf16[1,768,512]{2,1,0:T(8,128)(2,1)S(1)} %bitcast.73), channel_id=1, source_target_pairs={{0,8},{4,12},{1,9},{5,13},{2,10},{6,14},{3,11},{7,15},{16,24},{20,... | collective-permute-start | bytes 2359304 | tf_op jit(solution)/shard_map/ppermute | solution.py:20
  63.5 2.2 fusion.58
  65.8 26.5 %collective-permute-done = bf16[1,768,512]{2,1,0:T(8,128)(2,1)} collective-permute-done((bf16[1,768,512]{2,1,0:T(8,128)(2,1)S(1)}, bf16[1,768,512]{2,1,0:T(8,128)(2,1)}, u32[]{:S(2)}, u32[]{:S(2)}) %collective-permute-start) | collective-permute-done | bytes 786464 | tf_op jit(solution)/shard_map/ppermute | solution.py:20
  92.3 2.0 fusion.60
  94.3 2.3 fusion.36
  97.1 1.3 collective-permute-start.2
  98.9 4.8 %collective-permute-start.3 = (bf16[1,768,512]{1,2,0:T(8,128)(2,1)S(1)}, bf16[1,768,512]{1,2,0:T(8,128)(2,1)S(1)}, u32[]{:S(2)}, u32[]{:S(2)}) collective-permute-start(bf16[1,768,512]{1,2,0:T(8,128)(2,1)S(1)} %fusion.34), channel_id=1, source_target_pairs={{0,4},{4,8},{8,12},{1,5},{5,9},{9,13},{2,6},{6,10},{10,14},{3,7},{... | collective-permute-start | bytes 2359304 | tf_op jit(solution)/shard_map/ppermute | solution.py:20
  105.0 13.6 %collective-permute-done.2 = bf16[1,768,512]{1,2,0:T(8,128)(2,1)} collective-permute-done((bf16[1,768,512]{1,2,0:T(8,128)(2,1)S(1)}, bf16[1,768,512]{1,2,0:T(8,128)(2,1)}, u32[]{:S(2)}, u32[]{:S(2)}) %collective-permute-start.2) | collective-permute-done | bytes 786464 | tf_op jit(solution)/shard_map/ppermute | solution.py:20
  118.6 2.3 fusion.75
  121.0 1.2 fusion.69
  122.2 3.3 %maximum_multiply_fusion = f32[2304,768]{1,0:T(8,128)} fusion(f32[768,768]{1,0:T(8,128)S(1)} %fusion.69, f32[768,768]{1,0:T(8,128)S(1)} %fusion.72, f32[768,768]{1,0:T(8,128)S(1)} %fusion.75), kind=kLoop, calls=%fused_computation | loop fusion | flops 5308416 | bytes 14155776 | tf_op jit(solution)/shard_map/mul | solution.py:64
  125.5 3.3 %fusion.50 = f32[512,768]{1,0:T(8,128)} fusion(bf16[3,768,768]{2,1,0:T(8,128)(2,1)} %param.10, bf16[1,768,512]{1,2,0:T(8,128)(2,1)S(1)} %fusion.34), kind=kOutput, calls=%fused_computation.60 | convolution fusion | flops 603979776 | bytes 3538944 | tf_op jit(solution)/shard_map/co,sop->scp/dot_general | solution.py:47
  128.8 3.5 %fusion.52 = f32[512,768]{1,0:T(8,128)} fusion(bf16[3,768,768]{2,1,0:T(8,128)(2,1)} %param.10, bf16[1,768,512]{1,2,0:T(8,128)(2,1)} %collective-permute-done.2), kind=kOutput, calls=%fused_computation.62 | convolution fusion | flops 603979776 | bytes 3538944 | tf_op jit(solution)/shard_map/co,sop->scp/dot_general | solution.py:46
  132.3 117.0 %reduce-scatter.2.cloned.1.call-done = f32[576,768]{1,0:T(8,128)} async-done(((f32[2304,768]{1,0:T(8,128)}), f32[576,768]{1,0:T(8,128)}) %reduce-scatter.2.cloned.1.call-update) | async-done | bytes 1769488 | tf_op jit(solution)/shard_map/reduce_scatter | solution.py:114
  249.3 4.2 %fusion.41 = (f32[512]{0:T(512)S(1)}, f32[1,768,512]{1,2,0:T(8,128)S(1)}) fusion(bf16[1,768,512]{1,2,0:T(8,128)(2,1)S(1)} %copy.29, f32[768]{0:T(1024)S(1)} %copy-done.4, f32[512]{0:T(512)S(1)} %add_rsqrt_fusion, bf16[3,768,768]{2,1,0:T(8,128)(2,1)} %param.10, bf16[1,768,512]{1,2,0:T(8,128)(2,1)S(1)} %collective-permute-done.3, f32[512,768]{1,0:T(8,128)} %fusion.52, ...), kind=kOutput, calls=%fused_computation.53 | convolution fusion | flops 614202880 | bytes 7478272 | tf_op jit(solution)/shard_map/co,sop->scp/dot_general | solution.py:50
  255.2 43.0 %all-reduce.2.cloned.1.call-done = f32[576,768]{1,0:T(8,128)} async-done(((f32[576,768]{1,0:T(8,128)}), f32[576,768]{1,0:T(8,128)}) %all-reduce.2.cloned.1.call-update) | async-done | bytes 1769488 | tf_op jit(solution)/shard_map/psum | solution.py:115
  298.2 2.8 copy.32
  (32 shorter events, 6.2 us)
Async XLA Ops:
  7.2 242.1 %reduce-scatter.2.cloned.1.call-start = ((), (), s32[]{:S(2)}) async-start(), calls=%async_computation.2 | async-start | bytes 8847360 | tf_op jit(solution)/shard_map/reduce_scatter | solution.py:114
  54.7 1.6 copy-start
  54.9 37.4 %collective-permute-start = (bf16[1,768,512]{2,1,0:T(8,128)(2,1)S(1)}, bf16[1,768,512]{2,1,0:T(8,128)(2,1)}, u32[]{:S(2)}, u32[]{:S(2)}) collective-permute-start(bf16[1,768,512]{2,1,0:T(8,128)(2,1)S(1)} %bitcast.72), channel_id=1, source_target_pairs={{8,0},{12,4},{9,1},{13,5},{10,2},{14,6},{11,3},{15,7},{24,16},{28,... | collective-permute-start | bytes 2359304 | tf_op jit(solution)/shard_map/ppermute | solution.py:20
  56.8 37.4 %collective-permute-start.1 = (bf16[1,768,512]{2,1,0:T(8,128)(2,1)S(1)}, bf16[1,768,512]{2,1,0:T(8,128)(2,1)S(1)}, u32[]{:S(2)}, u32[]{:S(2)}) collective-permute-start(bf16[1,768,512]{2,1,0:T(8,128)(2,1)S(1)} %bitcast.73), channel_id=1, source_target_pairs={{0,8},{4,12},{1,9},{5,13},{2,10},{6,14},{3,11},{7,15},{16,24},{20,... | collective-permute-start | bytes 2359304 | tf_op jit(solution)/shard_map/ppermute | solution.py:20
  63.5 28.8 %copy-start.2 = (bf16[3,768,768]{2,1,0:T(8,128)(2,1)S(1)}, bf16[3,768,768]{2,1,0:T(8,128)(2,1)}, u32[]{:S(2)}) copy-start(bf16[3,768,768]{2,1,0:T(8,128)(2,1)} %param.11) | copy-start | bytes 10616836
  65.7 28.5 %copy-start.3 = (f32[768]{0:T(1024)S(1)}, f32[768]{0:T(1024)}, u32[]{:S(2)}) copy-start(f32[768]{0:T(1024)} %param.13) | copy-start | bytes 9220
  96.5 1.9 copy-start.1
  97.1 6.6 %copy-start.4 = (f32[768]{0:T(1024)S(1)}, f32[768]{0:T(1024)}, u32[]{:S(2)}) copy-start(f32[768]{0:T(1024)} %param.12) | copy-start | bytes 9220
  97.1 21.5 %collective-permute-start.2 = (bf16[1,768,512]{1,2,0:T(8,128)(2,1)S(1)}, bf16[1,768,512]{1,2,0:T(8,128)(2,1)}, u32[]{:S(2)}, u32[]{:S(2)}) collective-permute-start(bf16[1,768,512]{1,2,0:T(8,128)(2,1)S(1)} %fusion.34), channel_id=1, source_target_pairs={{4,0},{8,4},{12,8},{5,1},{9,5},{13,9},{6,2},{10,6},{14,10},{7,3},{... | collective-permute-start | bytes 2359304 | tf_op jit(solution)/shard_map/ppermute | solution.py:20
  98.9 22.0 %collective-permute-start.3 = (bf16[1,768,512]{1,2,0:T(8,128)(2,1)S(1)}, bf16[1,768,512]{1,2,0:T(8,128)(2,1)S(1)}, u32[]{:S(2)}, u32[]{:S(2)}) collective-permute-start(bf16[1,768,512]{1,2,0:T(8,128)(2,1)S(1)} %fusion.34), channel_id=1, source_target_pairs={{0,4},{4,8},{8,12},{1,5},{5,9},{9,13},{2,6},{6,10},{10,14},{3,7},{... | collective-permute-start | bytes 2359304 | tf_op jit(solution)/shard_map/ppermute | solution.py:20
  125.5 172.8 %all-reduce.2.cloned.1.call-start = ((), (), s32[]{:S(2)}) async-start(), calls=%async_computation.3 | async-start | bytes 3538944 | tf_op jit(solution)/shard_map/psum | solution.py:115
Sparse Core Ops, SparseCore 0:
  125.6 123.6 reduce-scatter.1
  251.7 46.5 all-reduce.1
where the time goes:
time: 308 us
  waiting for transfers between devices  200 us (65%)
  blocking collectives  26.3 us (9%)
  matrix products  22.2 us (7%)
  other arithmetic  16.5 us (5%)
  local copies, waits for them, and re-layouts  14.5 us (5%)
  between operations  14.3 us (5%)
  starting transfers between devices  13.9 us (5%)
    reduce_scatter x1, waiting for transfers between devices, on_device(): lax.psum_scatter(terms_one, 'seq', scatter_dimension=0, tiled=True)  117 us
    psum x1, waiting for transfers between devices, on_device(): first_weight_gradient = lax.psum(partial_rows, 'batch')  43 us
    ppermute x4, waiting for transfers between devices, shifted(): lax.ppermute(value, axis, [(source, source + steps) for source in range(i...  40.1 us
    all_to_all x1, blocking collectives, on_device(): lax.all_to_all(head_split_gradient, 'seq', split_axis=2, concat_axis=1, t...  26.3 us
    ppermute x4, starting transfers between devices, shifted(): lax.ppermute(value, axis, [(source, source + steps) for source in range(i...  13.9 us
    unnamed x18, local copies, waits for them, and re-layouts  12.3 us
    unnamed x1, other arithmetic  11.6 us
    dot_general x2, matrix products, input_grad(): jnp.einsum('co,sop->scp', weight[2], grad_lower, preferred_element_type=j...  6.43 us
  transfers between devices with their start and end apart: 6, of which 4 were waited for; matrix products, arithmetic and copies ran while one was open for 7% of the time, Pallas kernels for 0%

commit v1 on v0

v1 whole, which is shorter than its diff:
```python
import math

import jax
import jax.numpy as jnp
from jax import lax
from jax.experimental import pallas as pl
from jax.experimental.pallas import tpu as pltpu
from jax.sharding import PartitionSpec as P

DILATION_FIRST = 512
DILATION_SECOND = 1024


EPS = 1e-06
SLOPE = math.sqrt(2.0 / math.pi)
CUBIC = 0.044715
F32 = jnp.float32
BF16 = jnp.bfloat16


def shifted(value, axis, steps):
    count = lax.axis_size(axis)
    initial, last = (max(0, -steps), min(count, count - steps))
    return lax.ppermute(value, axis, [(source, source + steps) for source in range(initial, last)])


def gelu_slope(normed):
    inner = jnp.tanh(SLOPE * (normed + CUBIC * normed * normed * normed))
    return 0.5 * (1.0 + inner) + 0.5 * normed * (1.0 - inner * inner) * SLOPE * (
        1.0 + 3.0 * CUBIC * normed * normed
    )


def prepare(inputs, gain_vec):
    xfloat = inputs.astype(F32)
    meansq = jnp.mean(xfloat * xfloat, axis=1, keepdims=True)
    scale = lax.rsqrt(meansq + EPS)
    normed = xfloat * scale * gain_vec[None, :, None]
    gelu_out = jax.nn.gelu(normed, approximate=True).astype(BF16)
    return (xfloat, scale, normed, gelu_out)


def input_grad(xfloat, scale, normed, gain_vec, weight, grad_out, grad_upper, grad_lower):
    dgelu = jnp.einsum("co,sop->scp", weight[0], grad_upper, preferred_element_type=F32)
    dgelu = dgelu + jnp.einsum("co,sop->scp", weight[1], grad_out, preferred_element_type=F32)
    dgelu = dgelu + jnp.einsum("co,sop->scp", weight[2], grad_lower, preferred_element_type=F32)
    dnorm = dgelu * gelu_slope(normed) * gain_vec[None, :, None]
    inner = jnp.mean(dnorm * xfloat, axis=1, keepdims=True)
    dinput = scale * dnorm - xfloat * scale * scale * scale * inner
    return (grad_out.astype(F32) + dinput).astype(BF16)


def general(e_split, u_one, u_two, w_one, w_two, c_one, c_two):
    width = u_one.shape[2]
    factor = 1.0 / math.sqrt(
        u_one.shape[0] * lax.axis_size("batch") * width * lax.axis_size("seq")
    )
    e_two = lax.all_to_all(e_split, "seq", split_axis=2, concat_axis=1, tiled=True)
    span = DILATION_SECOND // width
    lower, upper = shifted(e_two, "seq", span), shifted(e_two, "seq", -span)
    xfloat, scale, normed, _ = prepare(u_two, c_two)
    e_one = input_grad(xfloat, scale, normed, c_two, w_two, e_two, upper, lower)
    span = DILATION_FIRST // width
    lower, upper = shifted(e_one, "seq", span), shifted(e_one, "seq", -span)
    xfloat, scale, normed, gelu_out = prepare(u_one, c_one)
    total = input_grad(xfloat, scale, normed, c_one, w_one, e_one, upper, lower)
    pieces = [
        jnp.einsum("scp,sop->co", gelu_out, tapped, preferred_element_type=F32)
        for tapped in (upper, e_one, lower)
    ]
    terms = jnp.concatenate(pieces, axis=0) * factor
    rows = lax.psum_scatter(terms, "seq", scatter_dimension=0, tiled=True)
    return (total, lax.psum(rows, "batch"))


def vmem():
    return pl.BlockSpec(memory_space=pltpu.VMEM)


def prep_kernel(with_gelu, u_ref, c_ref, q_ref, r_ref, *g_ref):
    u = u_ref[...].astype(F32)
    c = c_ref[...]
    r = lax.rsqrt(jnp.mean(u * u, axis=0, keepdims=True) + EPS)
    a = u * r * c
    inner = jnp.tanh(SLOPE * (a + CUBIC * a * a * a))
    slope = 0.5 * (1.0 + inner) + 0.5 * a * (1.0 - inner * inner) * SLOPE * (
        1.0 + 3.0 * CUBIC * a * a
    )
    q_ref[...] = slope * c
    r_ref[...] = r
    if with_gelu:
        g_ref[0][...] = (0.5 * a * (1.0 + inner)).astype(BF16)


def prep(u, c, with_gelu):
    chans, width = u.shape
    tile = 128
    block = pl.BlockSpec((chans, tile), lambda j: (0, j))
    shapes = [jax.ShapeDtypeStruct((chans, width), F32), jax.ShapeDtypeStruct((1, width), F32)]
    specs = [block, pl.BlockSpec((1, tile), lambda j: (0, j))]
    if with_gelu:
        shapes.append(jax.ShapeDtypeStruct((chans, width), BF16))
        specs.append(block)

    def body(*refs):
        prep_kernel(with_gelu, *refs)

    return pl.pallas_call(
        body,
        grid=(width // tile,),
        in_specs=[block, pl.BlockSpec((chans, 1), lambda j: (0, 0))],
        out_specs=specs,
        out_shape=shapes,
        cost_estimate=pl.CostEstimate(
            flops=30 * chans * width, bytes_accessed=8 * chans * width, transcendentals=chans * width
        ),
        name="prep_one" if with_gelu else "prep_two",
    )(u, c.reshape(chans, 1))


def finish(acc, e, u, q, r):
    dn = acc * q
    mean = jnp.mean(dn * u, axis=0, keepdims=True)
    return e + r * dn - u * (r * r * r * mean)


def middle(pieces, w, u, q, r, place):
    chans, width = u.shape
    part = pieces[0].shape[1]
    half = chans // 2
    tile = 256

    def body(place_ref, p0, p1, p2, p3, w_ref, u_ref, q_ref, r_ref, a_ref, b_ref, e_s, sems):
        me = place_ref[0]
        tap = place_ref[1]
        copies = []
        for k, piece in enumerate((p0, p1, p2, p3)):
            at = pl.multiple_of((me ^ k) * part, part)
            for j in range(2):
                copies.append(
                    pltpu.make_async_copy(
                        piece.at[j], e_s.at[j, pl.ds(at, part), :], sems.at[2 * k + j]
                    )
                )
        for copy in copies:
            copy.start()
        for copy in copies:
            copy.wait()
        for t in range(width // tile):
            cols = slice(t * tile, (t + 1) * tile)
            e = e_s[0, :, cols]
            acc = jnp.dot(w_ref[1], e, preferred_element_type=F32)
            acc = acc + jnp.dot(w_ref[tap], e_s[1, :, cols], preferred_element_type=F32)
            out = finish(
                acc, e.astype(F32), u_ref[:, cols].astype(F32), q_ref[:, cols], r_ref[:, cols]
            ).astype(BF16)
            a_ref[:, cols] = out[:half]
            b_ref[:, cols] = out[half:]

    return pl.pallas_call(
        body,
        in_specs=[pl.BlockSpec(memory_space=pltpu.SMEM)]
        + [pl.BlockSpec(memory_space=pl.ANY)] * 4
        + [vmem()] * 4,
        out_specs=[vmem()] * 2,
        out_shape=[jax.ShapeDtypeStruct((half, width), BF16)] * 2,
        scratch_shapes=[
            pltpu.VMEM((2, chans, width), BF16),
            pltpu.SemaphoreType.DMA((8,)),
        ],
        cost_estimate=pl.CostEstimate(
            flops=4 * chans * chans * width, bytes_accessed=10 * chans * width, transcendentals=0
        ),
        compiler_params=pltpu.CompilerParams(vmem_limit_bytes=40 << 20),
        name="middle",
    )(place, *pieces, w, u, q, r)


def taps(g, uppers, owns, lowers, place, factor, units, name):
    chans, width = g.shape
    cols = owns.shape[0]
    seq, halves = units
    unit = 3 * chans // (seq * halves * 2)
    grain = math.gcd(unit, chans)

    def body(place_ref, g_ref, up_ref, own_ref, low_ref, keep_ref, send_ref, acc_s, sem):
        core = place_ref[2]
        for tap, e_ref in enumerate((up_ref, own_ref, low_ref)):
            acc = lax.dot_general(
                g_ref[...], e_ref[...], (((1,), (1,)), ((), ())), preferred_element_type=F32
            )
            acc = acc * factor
            for j in range(chans // grain):
                row = tap * chans + j * grain
                n, off = divmod(row, unit)
                s, rest = divmod(n, 2 * halves)
                c, x = divmod(rest, halves)
                acc_s[c, x, s, off : off + grain, :] = acc[j * grain : (j + 1) * grain]
        copy = pltpu.make_async_copy(acc_s.at[core], keep_ref, sem)
        copy.start()
        send_ref[...] = acc_s[1 - core].astype(BF16)
        copy.wait()

    shape = (halves, seq, unit, cols)
    return pl.pallas_call(
        body,
        in_specs=[pl.BlockSpec(memory_space=pltpu.SMEM)] + [vmem()] * 4,
        out_specs=[pl.BlockSpec(memory_space=pl.ANY), vmem()],
        out_shape=[jax.ShapeDtypeStruct(shape, F32), jax.ShapeDtypeStruct(shape, BF16)],
        scratch_shapes=[pltpu.VMEM((2,) + shape, F32), pltpu.SemaphoreType.DMA],
        cost_estimate=pl.CostEstimate(
            flops=6 * chans * cols * width, bytes_accessed=12 * chans * cols, transcendentals=0
        ),
        compiler_params=pltpu.CompilerParams(vmem_limit_bytes=40 << 20),
        name=name,
    )(place, g, uppers, owns, lowers)


def last(uppers, owns, lowers, w, u, q, r):
    chans, width = u.shape
    half = chans // 2
    tile = 256

    def body(ua, ub, oa, ob, la, lb, w_ref, u_ref, q_ref, r_ref, out_ref):
        for t in range(width // tile):
            cols = slice(t * tile, (t + 1) * tile)
            acc = jnp.zeros((chans, tile), F32)
            for tap, (a, b) in enumerate(((ua, ub), (oa, ob), (la, lb))):
                e = jnp.concatenate([a[:, cols], b[:, cols]], axis=0)
                acc = acc + jnp.dot(w_ref[tap], e, preferred_element_type=F32)
            e = jnp.concatenate([oa[:, cols], ob[:, cols]], axis=0).astype(F32)
            out_ref[:, cols] = finish(
                acc, e, u_ref[:, cols].astype(F32), q_ref[:, cols], r_ref[:, cols]
            ).astype(BF16)

    return pl.pallas_call(
        body,
        in_specs=[vmem()] * 10,
        out_specs=vmem(),
        out_shape=jax.ShapeDtypeStruct((chans, width), BF16),
        cost_estimate=pl.CostEstimate(
            flops=6 * chans * chans * width, bytes_accessed=12 * chans * width, transcendentals=0
        ),
        compiler_params=pltpu.CompilerParams(vmem_limit_bytes=40 << 20),
        name="last",
    )(*uppers, *owns, *lowers, w, u, q, r)


def pairs(count, flip):
    return [(i, i ^ flip) for i in range(count)]


def pick(value, index):
    return lax.dynamic_index_in_dim(value, index, 0, keepdims=False)


def reduced(keep, send, seq, batch):
    core, x, me = lax.axis_index("batch") % 2, lax.axis_index("batch") // 2, lax.axis_index("seq")
    part = keep + lax.ppermute(send, "batch", pairs(batch, 1)).astype(F32)
    far = lax.ppermute(pick(part, 1 - x).astype(BF16), "batch", pairs(batch, 2))
    part = pick(part, x) + far.astype(F32)
    total = pick(part, me)
    moved = [
        lax.ppermute(pick(part, me ^ k).astype(BF16), "seq", pairs(seq, k)) for k in (3, 2, 1)
    ]
    for piece in moved:
        total = total + piece.astype(F32)
    mine = total.astype(BF16)
    other = lax.ppermute(mine, "batch", pairs(batch, 2))
    both = jnp.where(x == 0, jnp.stack([mine, other]), jnp.stack([other, mine]))
    other = lax.ppermute(both, "batch", pairs(batch, 1))
    full = jnp.where(core == 0, jnp.stack([both, other]), jnp.stack([other, both]))
    return full.astype(F32).reshape(-1, mine.shape[-1])


def four_shards(e_split, u_one, u_two, w_one, w_two, c_one, c_two):
    seq, batch = lax.axis_size("seq"), lax.axis_size("batch")
    me = lax.axis_index("seq")
    core = lax.axis_index("batch") % 2
    e_split, u_one, u_two = e_split[0], u_one[0], u_two[0]
    chans, width = u_one.shape
    part = e_split.shape[0]
    factor = 1.0 / math.sqrt(batch * width * seq)

    def block(index):
        return lax.dynamic_slice(e_split, (0, index * width), (part, width))

    pieces = [jnp.stack([block(me ^ k), block(me ^ k ^ 2)]) for k in range(4)]
    for k in (3, 2, 1):
        pieces[k] = lax.ppermute(pieces[k], "seq", pairs(seq, k))
    place = jnp.stack([me, jnp.where(me < 2, 0, 2), core]).astype(jnp.int32)
    q_two, r_two = prep(u_two, c_two, False)
    q_one, r_one, g_one = prep(u_one, c_one, True)
    owns = middle(pieces, w_two, u_two, q_two, r_two, place)
    lowers = [shifted(e, "seq", 1) for e in owns]
    uppers = [shifted(e, "seq", -1) for e in owns]
    chunks = []
    for j in range(2):
        keep, send = taps(
            g_one, uppers[j], owns[j], lowers[j], place, factor, (seq, 2), f"taps_{j}"
        )
        chunks.append(reduced(keep, send, seq, batch))
    total = last(uppers, owns, lowers, w_one, u_one, q_one, r_one)
    return (total[None], jnp.concatenate(chunks, axis=1))


def on_device(e_split, u_one, u_two, *rest):
    width = u_one.shape[2]
    fits = (
        lax.axis_size("seq") == 4
        and lax.axis_size("batch") == 4
        and width == DILATION_FIRST
        and 2 * width == DILATION_SECOND
        and u_one.shape[0] == 1
    )
    return (four_shards if fits else general)(e_split, u_one, u_two, *rest)


def solution(mesh):
    in_specs = (
        P(("grp", "batch"), "seq", None),
        P(("grp", "batch"), None, "seq"),
        P(("grp", "batch"), None, "seq"),
        P(),
        P(),
        P(),
        P(),
    )
    out_specs = (P(("grp", "batch"), None, "seq"), P(("grp", "seq"), None))
    return jax.shard_map(
        on_device, mesh=mesh, in_specs=in_specs, out_specs=out_specs, check_vma=False
    )
```

time: 308 us -> 127 us (0.41)
  waiting for transfers between devices: 200 us -> 42.2 us
  blocking collectives: 26.3 us -> 0 us
  starting transfers between devices: 13.9 us -> 39.6 us
  Pallas kernels: 0 us -> 25.5 us
  matrix products: 22.2 us -> 0 us
  between operations: 14.3 us -> 1.13 us
  other arithmetic: 16.5 us -> 7.44 us
  local copies, waits for them, and re-layouts: 14.5 us -> 10 us
    reduce_scatter x1 -> x0, waiting for transfers between devices: 117 us -> none  [on_device(): lax.psum_scatter(terms_one, 'seq', scatter_dimension=0, tiled=True)]
    psum x1 -> x0, waiting for transfers between devices: 43 us -> none  [on_device(): first_weight_gradient = lax.psum(partial_rows, 'batch')]
    ppermute x0 -> x17, waiting for transfers between devices: none -> 40.6 us  [the longest x3 21.3 us: four_shards(): pieces[k] = lax.ppermute(pieces[k], 'seq', pairs(seq, k))]
    ppermute x4, waiting for transfers between devices: 40.1 us -> 1.63 us  [shifted(): lax.ppermute(value, axis, [(source, source + steps) for source in range(i...]
    all_to_all x1 -> x0, blocking collectives: 26.3 us -> none  [on_device(): lax.all_to_all(head_split_gradient, 'seq', split_axis=2, concat_axis=1, t...]
    pallas_call x0 -> x6, Pallas kernels: none -> 25.5 us  [the longest x2 8.96 us: prep(): pl.pallas_call(body, grid=(width // tile,), in_specs=[block, pl.BlockSpec...]
    dot_general x9 -> x0, matrix products: 22.2 us -> none  [the longest x2 6.43 us: input_grad(): jnp.einsum('co,sop->scp', weight[2], grad_lower, preferred_element_type=j...]
    ppermute x0 -> x17, starting transfers between devices: none -> 22.1 us  [the longest x6 10.4 us: reduced(): lax.ppermute(pick(part, me ^ k).astype(BF16), 'seq', pairs(seq, k))]
  transfers between devices with their start and end apart: 6 -> 21, of which waited for: 4 -> 10; matrix products, arithmetic and copies ran while one was open for 7% -> 6% of each run, Pallas kernels for 0% -> 16%
where the time goes in v1:
time: 127 us; the launch traced here: 126 us
  waiting for transfers between devices  42.2 us (33%)
  starting transfers between devices  39.6 us (31%)
  Pallas kernels  25.5 us (20%)
  local copies, waits for them, and re-layouts  10 us (8%)
  other arithmetic  7.44 us (6%)
    ppermute x3, waiting for transfers between devices, four_shards(): pieces[k] = lax.ppermute(pieces[k], 'seq', pairs(seq, k))  21.3 us
    ppermute x4, starting transfers between devices, shifted(): lax.ppermute(value, axis, [(source, source + steps) for source in range(i...  17.4 us
    ppermute x6, starting transfers between devices, reduced(): lax.ppermute(pick(part, me ^ k).astype(BF16), 'seq', pairs(seq, k))  10.4 us
    pallas_call x2, Pallas kernels, prep(): pl.pallas_call(body, grid=(width // tile,), in_specs=[block, pl.BlockSpec...  8.96 us
    ppermute x2, waiting for transfers between devices, reduced(): far = lax.ppermute(pick(part, 1 - x).astype(BF16), 'batch', pairs(batch, 2))  8.09 us
    pallas_call x2, Pallas kernels, taps(): pl.pallas_call(body, in_specs=[pl.BlockSpec(memory_space=pltpu.SMEM)] + [...  7.17 us
    ppermute x6, waiting for transfers between devices, reduced(): lax.ppermute(pick(part, me ^ k).astype(BF16), 'seq', pairs(seq, k))  6.78 us
    unnamed x46, local copies, waits for them, and re-layouts  6.44 us
  transfers between devices with their start and end apart: 21, of which 10 were waited for; matrix products, arithmetic and copies ran while one was open for 6% of the time, Pallas kernels for 16%

profile of v1, /device:TPU:0, one launch (start us, length us, event | category | flops | bytes accessed | tf_op | source)
XLA Modules:
  0.0 125.9 jit_solution(2006290674860287738)
XLA Ops:
  0.7 1.5 %constant_dynamic-slice_fusion.1 = (bf16[1,192,512]{2,1,0:T(8,128)(2,1)S(1)}, bf16[1,192,512]{2,1,0:T(8,128)(2,1)S(1)}, bf16[1,192,512]{2,1,0:T(8,128)(2,1)S(1)}...) fusion(bf16[1,192,2048]{2,1,0:T(8,128)(2,1)} %param.7, ...), kind=kLoop, calls=%fused_computation.40 | loop fusion | bytes 2752540 | tf_op jit(solution)/shard_map/dynamic_slice | solution.py:286
  3.0 3.1 %collective-permute-start = (bf16[2,192,512]{2,1,0:T(8,128)(2,1)}, bf16[2,192,512]{2,1,0:T(8,128)(2,1)}, u32[]{:S(2)}, u32[]{:S(2)}) collective-permute-start(bf16[2,192,512]{2,1,0:T(8,128)(2,1)} %pad_maximum_fusion.1), channel_id=1, source_target_pairs={{0,4},{4,0},{8,12},{12,8},{1,5},{5,1},{9,13},{13,9},{2,6},{6,2},{1... | collective-permute-start | bytes 1179656 | tf_op jit(solution)/shard_map/ppermute | solution.py:290
  7.0 2.6 %collective-permute-start.1 = (bf16[2,192,512]{2,1,0:T(8,128)(2,1)}, bf16[2,192,512]{2,1,0:T(8,128)(2,1)}, u32[]{:S(2)}, u32[]{:S(2)}) collective-permute-start(bf16[2,192,512]{2,1,0:T(8,128)(2,1)} %get-tuple-element.37), channel_id=1, source_target_pairs={{0,8},{4,12},{8,0},{12,4},{1,9},{5,13},{9,1},{13,5},{2,10},{6,14},... | collective-permute-start | bytes 1179656 | tf_op jit(solution)/shard_map/ppermute | solution.py:290
  11.3 4.4 %prep_two.1 = (f32[768,512]{1,0:T(8,128)}, f32[1,512]{1,0:T(1,128)}) custom-call(bf16[768,512]{1,0:T(8,128)(2,1)} %bitcast.56, f32[768,1]{1,0:T(8,128)} %reshape.166.refs_1_), custom_call_target="tpu_custom_call" | custom-call | flops 11796480 | bytes 3145728 | tf_op jit(solution)/shard_map/prep_two/pallas_call | solution.py:108
  15.8 6.9 %collective-permute-done.p1 = bf16[2,192,512]{2,1,0:T(8,128)(2,1)} collective-permute-done((bf16[2,192,512]{2,1,0:T(8,128)(2,1)}, bf16[2,192,512]{2,1,0:T(8,128)(2,1)}, u32[]{:S(2)}, u32[]{:S(2)}) %collective-permute-start) | collective-permute-done | bytes 393248 | tf_op jit(solution)/shard_map/ppermute | solution.py:290
  22.7 14.3 %collective-permute-done.1.p2 = bf16[2,192,512]{2,1,0:T(8,128)(2,1)} collective-permute-done((bf16[2,192,512]{2,1,0:T(8,128)(2,1)}, bf16[2,192,512]{2,1,0:T(8,128)(2,1)}, u32[]{:S(2)}, u32[]{:S(2)}) %collective-permute-start.1) | collective-permute-done | bytes 393248 | tf_op jit(solution)/shard_map/ppermute | solution.py:290
  41.3 5.0 %middle.1 = (bf16[384,512]{1,0:T(8,128)(2,1)S(1)}, bf16[384,512]{1,0:T(8,128)(2,1)}) custom-call(s32[3]{0:T(128)S(1)} %pad_add_fusion.place_ref, bf16[2,192,512]{2,1,0:T(8,128)(2,1)S(1)} %copy-done.4, bf16[2,192,512]{2,1,0:T(8,128)(2,1)} %collective-permute-done.p1, bf16[2,192,512]{2,1,0:T(8,128)(2,1)} %collective-permute-done.1.p2, ...), custom_call_target="tpu_custom_call" | custom-call | flops 1207959552 | bytes 3932160 | tf_op jit(solution)/shard_map/middle/pallas_call | solution.py:160
  48.4 10.2 %collective-permute-start.6 = (bf16[384,512]{1,0:T(8,128)(2,1)}, bf16[384,512]{1,0:T(8,128)(2,1)S(1)}, u32[]{:S(2)}, u32[]{:S(2)}) collective-permute-start(bf16[384,512]{1,0:T(8,128)(2,1)} %get-tuple-element.16.ob.own_ref), channel_id=1, source_target_pairs={{0,4},{4,8},{8,12},{1,5},{5,9},{9,13},{2,6},{6,10},{10,14},{3,7},{... | collective-permute-start | bytes 1179656 | tf_op jit(solution)/shard_map/ppermute | solution.py:24
  59.5 4.6 %prep_one.1 = (f32[768,512]{1,0:T(8,128)}, f32[1,512]{1,0:T(1,128)}, bf16[768,512]{1,0:T(8,128)(2,1)}) custom-call(bf16[768,512]{1,0:T(8,128)(2,1)} %bitcast.54, f32[768,1]{1,0:T(8,128)} %reshape.167.refs_1_), custom_call_target="tpu_custom_call" | custom-call | flops 11796480 | bytes 3145728 | tf_op jit(solution)/shard_map/prep_one/pallas_call | solution.py:108
  65.5 4.6 %collective-permute-start.5 = (bf16[384,512]{1,0:T(8,128)(2,1)}, bf16[384,512]{1,0:T(8,128)(2,1)S(1)}, u32[]{:S(2)}, u32[]{:S(2)}) collective-permute-start(bf16[384,512]{1,0:T(8,128)(2,1)} %copy-done.7), channel_id=1, source_target_pairs={{0,4},{4,8},{8,12},{1,5},{5,9},{9,13},{2,6},{6,10},{10,14},{3,7},{... | collective-permute-start | bytes 1179656 | tf_op jit(solution)/shard_map/ppermute | solution.py:24
  71.5 3.8 %taps_1.1 = (f32[2,4,144,384]{3,2,1,0:T(8,128)S(1)}, bf16[2,4,144,384]{3,2,1,0:T(8,128)(2,1)}) custom-call(s32[3]{0:T(128)S(1)} %pad_add_fusion.place_ref, bf16[768,512]{1,0:T(8,128)(2,1)S(1)} %copy-done.20, bf16[384,512]{1,0:T(8,128)(2,1)S(1)} %collective-permute-done.4.ub.up_ref, bf16[384,512]{1,0:T(8,128)(2,1)} %get-tuple-element.16.ob.own_ref, ...), custom_call_target="tpu_custom_call" | custom-call | flops 905969664 | bytes 3538944 | tf_op jit(solution)/shard_map/taps_1/pallas_call | solution.py:205
  77.1 3.3 %taps_0.1 = (f32[2,4,144,384]{3,2,1,0:T(8,128)S(1)}, bf16[2,4,144,384]{3,2,1,0:T(8,128)(2,1)}) custom-call(s32[3]{0:T(128)S(1)} %pad_add_fusion.place_ref, bf16[768,512]{1,0:T(8,128)(2,1)S(1)} %copy-done.20, bf16[384,512]{1,0:T(8,128)(2,1)S(1)} %collective-permute-done.3.ua.up_ref, bf16[384,512]{1,0:T(8,128)(2,1)S(1)} %copy-done.8, ...), custom_call_target="tpu_custom_call" | custom-call | flops 905969664 | bytes 3538944 | tf_op jit(solution)/shard_map/taps_0/pallas_call | solution.py:205
  82.2 1.6 %collective-permute-start.15 = (bf16[4,144,384]{2,1,0:T(8,128)(2,1)S(1)}, bf16[4,144,384]{2,1,0:T(8,128)(2,1)S(1)}, u32[]{:S(2)}, u32[]{:S(2)}) collective-permute-start(bf16[4,144,384]{2,1,0:T(8,128)(2,1)S(1)} %fusion.1), channel_id=1, source_target_pairs={{0,2},{1,3},{2,0},{3,1},{4,6},{5,7},{6,4},{7,5},{8,10},{9,11},{10,... | collective-permute-start | bytes 1327112 | tf_op jit(solution)/shard_map/ppermute | solution.py:260
  86.5 4.3 %last.1 = bf16[768,512]{1,0:T(8,128)(2,1)} custom-call(bf16[384,512]{1,0:T(8,128)(2,1)S(1)} %copy-done.15, bf16[384,512]{1,0:T(8,128)(2,1)S(1)} %copy-done.11, bf16[384,512]{1,0:T(8,128)(2,1)S(1)} %copy-done.9, bf16[384,512]{1,0:T(8,128)(2,1)} %get-tuple-element.16.ob.own_ref, bf16[384,512]{1,0:T(8,128)(2,1)S(1)} %copy-done.17, ...), custom_call_target="tpu_custom_call" | custom-call | flops 1811939328 | bytes 4718592 | tf_op jit(solution)/shard_map/last/pallas_call | solution.py:236
  90.8 4.5 %collective-permute-done.15 = bf16[4,144,384]{2,1,0:T(8,128)(2,1)S(1)} collective-permute-done((bf16[4,144,384]{2,1,0:T(8,128)(2,1)S(1)}, bf16[4,144,384]{2,1,0:T(8,128)(2,1)S(1)}, u32[]{:S(2)}, u32[]{:S(2)}) %collective-permute-start.15) | collective-permute-done | bytes 442400 | tf_op jit(solution)/shard_map/ppermute | solution.py:260
  95.4 2.4 %collective-permute-start.18 = (bf16[144,384]{1,0:T(8,128)(2,1)S(1)}, bf16[144,384]{1,0:T(8,128)(2,1)S(1)}, u32[]{:S(2)}, u32[]{:S(2)}) collective-permute-start(bf16[144,384]{1,0:T(8,128)(2,1)S(1)} %get-tuple-element.28), channel_id=1, source_target_pairs={{0,4},{4,0},{8,12},{12,8},{1,5},{5,1},{9,13},{13,9},{2,6},{6,2},{1... | collective-permute-start | bytes 331784 | tf_op jit(solution)/shard_map/ppermute | solution.py:264
  97.9 2.8 %collective-permute-start.17 = (bf16[144,384]{1,0:T(8,128)(2,1)S(1)}, bf16[144,384]{1,0:T(8,128)(2,1)S(1)}, u32[]{:S(2)}, u32[]{:S(2)}) collective-permute-start(bf16[144,384]{1,0:T(8,128)(2,1)S(1)} %get-tuple-element.29), channel_id=1, source_target_pairs={{0,8},{4,12},{8,0},{12,4},{1,9},{5,13},{9,1},{13,5},{2,10},{6,14},... | collective-permute-start | bytes 331784 | tf_op jit(solution)/shard_map/ppermute | solution.py:264
  100.7 3.6 %collective-permute-done.8 = bf16[4,144,384]{2,1,0:T(8,128)(2,1)S(1)} collective-permute-done((bf16[4,144,384]{2,1,0:T(8,128)(2,1)S(1)}, bf16[4,144,384]{2,1,0:T(8,128)(2,1)S(1)}, u32[]{:S(2)}, u32[]{:S(2)}) %collective-permute-start.8) | collective-permute-done | bytes 442400 | tf_op jit(solution)/shard_map/ppermute | solution.py:260
  104.4 2.4 %collective-permute-start.11 = (bf16[144,384]{1,0:T(8,128)(2,1)S(1)}, bf16[144,384]{1,0:T(8,128)(2,1)S(1)}, u32[]{:S(2)}, u32[]{:S(2)}) collective-permute-start(bf16[144,384]{1,0:T(8,128)(2,1)S(1)} %get-tuple-element.25), channel_id=1, source_target_pairs={{0,4},{4,0},{8,12},{12,8},{1,5},{5,1},{9,13},{13,9},{2,6},{6,2},{1... | collective-permute-start | bytes 331784 | tf_op jit(solution)/shard_map/ppermute | solution.py:264
  106.8 2.8 %collective-permute-start.10 = (bf16[144,384]{1,0:T(8,128)(2,1)S(1)}, bf16[144,384]{1,0:T(8,128)(2,1)S(1)}, u32[]{:S(2)}, u32[]{:S(2)}) collective-permute-start(bf16[144,384]{1,0:T(8,128)(2,1)S(1)} %get-tuple-element.26), channel_id=1, source_target_pairs={{0,8},{4,12},{8,0},{12,4},{1,9},{5,13},{9,1},{13,5},{2,10},{6,14},... | collective-permute-start | bytes 331784 | tf_op jit(solution)/shard_map/ppermute | solution.py:264
  109.7 1.6 %collective-permute-start.19 = (bf16[144,384]{1,0:T(8,128)(2,1)S(1)}, bf16[144,384]{1,0:T(8,128)(2,1)S(1)}, u32[]{:S(2)}, u32[]{:S(2)}) collective-permute-start(bf16[144,384]{1,0:T(8,128)(2,1)S(1)} %fusion.4), channel_id=1, source_target_pairs={{0,2},{1,3},{2,0},{3,1},{4,6},{5,7},{6,4},{7,5},{8,10},{9,11},{10,... | collective-permute-start | bytes 331784 | tf_op jit(solution)/shard_map/ppermute | solution.py:269
  111.5 6.5 %collective-permute-done.10 = bf16[144,384]{1,0:T(8,128)(2,1)S(1)} collective-permute-done((bf16[144,384]{1,0:T(8,128)(2,1)S(1)}, bf16[144,384]{1,0:T(8,128)(2,1)S(1)}, u32[]{:S(2)}, u32[]{:S(2)}) %collective-permute-start.10) | collective-permute-done | bytes 110624 | tf_op jit(solution)/shard_map/ppermute | solution.py:264
  118.1 1.6 %collective-permute-start.12 = (bf16[144,384]{1,0:T(8,128)(2,1)S(1)}, bf16[144,384]{1,0:T(8,128)(2,1)S(1)}, u32[]{:S(2)}, u32[]{:S(2)}) collective-permute-start(bf16[144,384]{1,0:T(8,128)(2,1)S(1)} %fusion.7), channel_id=1, source_target_pairs={{0,2},{1,3},{2,0},{3,1},{4,6},{5,7},{6,4},{7,5},{8,10},{9,11},{10,... | collective-permute-start | bytes 331784 | tf_op jit(solution)/shard_map/ppermute | solution.py:269
  119.7 3.1 %collective-permute-done.12 = bf16[144,384]{1,0:T(8,128)(2,1)S(1)} collective-permute-done((bf16[144,384]{1,0:T(8,128)(2,1)S(1)}, bf16[144,384]{1,0:T(8,128)(2,1)S(1)}, u32[]{:S(2)}, u32[]{:S(2)}) %collective-permute-start.12) | collective-permute-done | bytes 110624 | tf_op jit(solution)/shard_map/ppermute | solution.py:269
  (94 shorter events, 23.2 us)
Async XLA Ops:
  3.0 19.7 %collective-permute-start = (bf16[2,192,512]{2,1,0:T(8,128)(2,1)}, bf16[2,192,512]{2,1,0:T(8,128)(2,1)}, u32[]{:S(2)}, u32[]{:S(2)}) collective-permute-start(bf16[2,192,512]{2,1,0:T(8,128)(2,1)} %pad_maximum_fusion.1), channel_id=1, source_target_pairs={{0,4},{4,0},{8,12},{12,8},{1,5},{5,1},{9,13},{13,9},{2,6},{6,2},{1... | collective-permute-start | bytes 1179656 | tf_op jit(solution)/shard_map/ppermute | solution.py:290
  6.1 31.0 %copy-start = (bf16[3,768,768]{2,1,0:T(8,128)(2,1)S(1)}, bf16[3,768,768]{2,1,0:T(8,128)(2,1)}, u32[]{:S(2)}) copy-start(bf16[3,768,768]{2,1,0:T(8,128)(2,1)} %w_ref.2) | copy-start | bytes 10616836
  7.0 30.1 %collective-permute-start.1 = (bf16[2,192,512]{2,1,0:T(8,128)(2,1)}, bf16[2,192,512]{2,1,0:T(8,128)(2,1)}, u32[]{:S(2)}, u32[]{:S(2)}) collective-permute-start(bf16[2,192,512]{2,1,0:T(8,128)(2,1)} %get-tuple-element.37), channel_id=1, source_target_pairs={{0,8},{4,12},{8,0},{12,4},{1,9},{5,13},{9,1},{13,5},{2,10},{6,14},... | collective-permute-start | bytes 1179656 | tf_op jit(solution)/shard_map/ppermute | solution.py:290
  10.4 26.7 %collective-permute-start.2 = (bf16[2,192,512]{2,1,0:T(8,128)(2,1)}, bf16[2,192,512]{2,1,0:T(8,128)(2,1)}, u32[]{:S(2)}, u32[]{:S(2)}) collective-permute-start(bf16[2,192,512]{2,1,0:T(8,128)(2,1)} %pad_maximum_fusion.3), channel_id=1, source_target_pairs={{0,12},{4,8},{8,4},{12,0},{1,13},{5,9},{9,5},{13,1},{2,14},{6,10},... | collective-permute-start | bytes 1179656 | tf_op jit(solution)/shard_map/ppermute | solution.py:290
  41.3 17.3 %copy-start.22 = (f32[768]{0:T(1024)S(1)}, f32[768]{0:T(1024)}, u32[]{:S(2)}) copy-start(f32[768]{0:T(1024)} %param.12) | copy-start | bytes 9220
  47.1 23.0 %collective-permute-start.4 = (bf16[384,512]{1,0:T(8,128)(2,1)}, bf16[384,512]{1,0:T(8,128)(2,1)S(1)}, u32[]{:S(2)}, u32[]{:S(2)}) collective-permute-start(bf16[384,512]{1,0:T(8,128)(2,1)} %get-tuple-element.16.ob.own_ref), channel_id=1, source_target_pairs={{4,0},{8,4},{12,8},{5,1},{9,5},{13,9},{6,2},{10,6},{14,10},{7,3},{... | collective-permute-start | bytes 1179656 | tf_op jit(solution)/shard_map/ppermute | solution.py:24
  48.4 21.7 %collective-permute-start.6 = (bf16[384,512]{1,0:T(8,128)(2,1)}, bf16[384,512]{1,0:T(8,128)(2,1)S(1)}, u32[]{:S(2)}, u32[]{:S(2)}) collective-permute-start(bf16[384,512]{1,0:T(8,128)(2,1)} %get-tuple-element.16.ob.own_ref), channel_id=1, source_target_pairs={{0,4},{4,8},{8,12},{1,5},{5,9},{9,13},{2,6},{6,10},{10,14},{3,7},{... | collective-permute-start | bytes 1179656 | tf_op jit(solution)/shard_map/ppermute | solution.py:24
  64.1 13.0 %copy-start.8 = (bf16[384,512]{1,0:T(8,128)(2,1)S(1)}, bf16[384,512]{1,0:T(8,128)(2,1)}, u32[]{:S(2)}) copy-start(bf16[384,512]{1,0:T(8,128)(2,1)} %copy-done.7) | copy-start | bytes 1179652
  64.1 11.7 %collective-permute-start.3 = (bf16[384,512]{1,0:T(8,128)(2,1)}, bf16[384,512]{1,0:T(8,128)(2,1)S(1)}, u32[]{:S(2)}, u32[]{:S(2)}) collective-permute-start(bf16[384,512]{1,0:T(8,128)(2,1)} %copy-done.7), channel_id=1, source_target_pairs={{4,0},{8,4},{12,8},{5,1},{9,5},{13,9},{6,2},{10,6},{14,10},{7,3},{... | collective-permute-start | bytes 1179656 | tf_op jit(solution)/shard_map/ppermute | solution.py:24
  65.5 11.6 %collective-permute-start.5 = (bf16[384,512]{1,0:T(8,128)(2,1)}, bf16[384,512]{1,0:T(8,128)(2,1)S(1)}, u32[]{:S(2)}, u32[]{:S(2)}) collective-permute-start(bf16[384,512]{1,0:T(8,128)(2,1)} %copy-done.7), channel_id=1, source_target_pairs={{0,4},{4,8},{8,12},{1,5},{5,9},{9,13},{2,6},{6,10},{10,14},{3,7},{... | collective-permute-start | bytes 1179656 | tf_op jit(solution)/shard_map/ppermute | solution.py:24
  75.4 5.2 %collective-permute-start.14 = (bf16[2,4,144,384]{3,2,1,0:T(8,128)(2,1)}, bf16[2,4,144,384]{3,2,1,0:T(8,128)(2,1)}, u32[]{:S(2)}, u32[]{:S(2)}) collective-permute-start(bf16[2,4,144,384]{3,2,1,0:T(8,128)(2,1)} %get-tuple-element.23), channel_id=1, source_target_pairs={{0,1},{1,0},{2,3},{3,2},{4,5},{5,4},{6,7},{7,6},{8,9},{9,8},{10,11... | collective-permute-start | bytes 2654216 | tf_op jit(solution)/shard_map/ppermute | solution.py:259
  80.5 3.3 %collective-permute-start.7 = (bf16[2,4,144,384]{3,2,1,0:T(8,128)(2,1)}, bf16[2,4,144,384]{3,2,1,0:T(8,128)(2,1)}, u32[]{:S(2)}, u32[]{:S(2)}) collective-permute-start(bf16[2,4,144,384]{3,2,1,0:T(8,128)(2,1)} %get-tuple-element.21), channel_id=1, source_target_pairs={{0,1},{1,0},{2,3},{3,2},{4,5},{5,4},{6,7},{7,6},{8,9},{9,8},{10,11... | collective-permute-start | bytes 2654216 | tf_op jit(solution)/shard_map/ppermute | solution.py:259
  82.2 13.1 %collective-permute-start.15 = (bf16[4,144,384]{2,1,0:T(8,128)(2,1)S(1)}, bf16[4,144,384]{2,1,0:T(8,128)(2,1)S(1)}, u32[]{:S(2)}, u32[]{:S(2)}) collective-permute-start(bf16[4,144,384]{2,1,0:T(8,128)(2,1)S(1)} %fusion.1), channel_id=1, source_target_pairs={{0,2},{1,3},{2,0},{3,1},{4,6},{5,7},{6,4},{7,5},{8,10},{9,11},{10,... | collective-permute-start | bytes 1327112 | tf_op jit(solution)/shard_map/ppermute | solution.py:260
  85.3 18.9 %collective-permute-start.8 = (bf16[4,144,384]{2,1,0:T(8,128)(2,1)S(1)}, bf16[4,144,384]{2,1,0:T(8,128)(2,1)S(1)}, u32[]{:S(2)}, u32[]{:S(2)}) collective-permute-start(bf16[4,144,384]{2,1,0:T(8,128)(2,1)S(1)} %fusion), channel_id=1, source_target_pairs={{0,2},{1,3},{2,0},{3,1},{4,6},{5,7},{6,4},{7,5},{8,10},{9,11},{10,... | collective-permute-start | bytes 1327112 | tf_op jit(solution)/shard_map/ppermute | solution.py:260
  95.4 14.1 %collective-permute-start.18 = (bf16[144,384]{1,0:T(8,128)(2,1)S(1)}, bf16[144,384]{1,0:T(8,128)(2,1)S(1)}, u32[]{:S(2)}, u32[]{:S(2)}) collective-permute-start(bf16[144,384]{1,0:T(8,128)(2,1)S(1)} %get-tuple-element.28), channel_id=1, source_target_pairs={{0,4},{4,0},{8,12},{12,8},{1,5},{5,1},{9,13},{13,9},{2,6},{6,2},{1... | collective-permute-start | bytes 331784 | tf_op jit(solution)/shard_map/ppermute | solution.py:264
  97.9 11.7 %collective-permute-start.17 = (bf16[144,384]{1,0:T(8,128)(2,1)S(1)}, bf16[144,384]{1,0:T(8,128)(2,1)S(1)}, u32[]{:S(2)}, u32[]{:S(2)}) collective-permute-start(bf16[144,384]{1,0:T(8,128)(2,1)S(1)} %get-tuple-element.29), channel_id=1, source_target_pairs={{0,8},{4,12},{8,0},{12,4},{1,9},{5,13},{9,1},{13,5},{2,10},{6,14},... | collective-permute-start | bytes 331784 | tf_op jit(solution)/shard_map/ppermute | solution.py:264
  100.6 8.9 %collective-permute-start.16 = (bf16[144,384]{1,0:T(8,128)(2,1)S(1)}, bf16[144,384]{1,0:T(8,128)(2,1)S(1)}, u32[]{:S(2)}, u32[]{:S(2)}) collective-permute-start(bf16[144,384]{1,0:T(8,128)(2,1)S(1)} %get-tuple-element.27), channel_id=1, source_target_pairs={{0,12},{4,8},{8,4},{12,0},{1,13},{5,9},{9,5},{13,1},{2,14},{6,10},... | collective-permute-start | bytes 331784 | tf_op jit(solution)/shard_map/ppermute | solution.py:264
  104.4 7.1 %collective-permute-start.11 = (bf16[144,384]{1,0:T(8,128)(2,1)S(1)}, bf16[144,384]{1,0:T(8,128)(2,1)S(1)}, u32[]{:S(2)}, u32[]{:S(2)}) collective-permute-start(bf16[144,384]{1,0:T(8,128)(2,1)S(1)} %get-tuple-element.25), channel_id=1, source_target_pairs={{0,4},{4,0},{8,12},{12,8},{1,5},{5,1},{9,13},{13,9},{2,6},{6,2},{1... | collective-permute-start | bytes 331784 | tf_op jit(solution)/shard_map/ppermute | solution.py:264
  106.8 11.2 %collective-permute-start.10 = (bf16[144,384]{1,0:T(8,128)(2,1)S(1)}, bf16[144,384]{1,0:T(8,128)(2,1)S(1)}, u32[]{:S(2)}, u32[]{:S(2)}) collective-permute-start(bf16[144,384]{1,0:T(8,128)(2,1)S(1)} %get-tuple-element.26), channel_id=1, source_target_pairs={{0,8},{4,12},{8,0},{12,4},{1,9},{5,13},{9,1},{13,5},{2,10},{6,14},... | collective-permute-start | bytes 331784 | tf_op jit(solution)/shard_map/ppermute | solution.py:264
  109.6 8.4 %collective-permute-start.9 = (bf16[144,384]{1,0:T(8,128)(2,1)S(1)}, bf16[144,384]{1,0:T(8,128)(2,1)S(1)}, u32[]{:S(2)}, u32[]{:S(2)}) collective-permute-start(bf16[144,384]{1,0:T(8,128)(2,1)S(1)} %get-tuple-element.24), channel_id=1, source_target_pairs={{0,12},{4,8},{8,4},{12,0},{1,13},{5,9},{9,5},{13,1},{2,14},{6,10},... | collective-permute-start | bytes 331784 | tf_op jit(solution)/shard_map/ppermute | solution.py:264
  109.7 10.0 %collective-permute-start.19 = (bf16[144,384]{1,0:T(8,128)(2,1)S(1)}, bf16[144,384]{1,0:T(8,128)(2,1)S(1)}, u32[]{:S(2)}, u32[]{:S(2)}) collective-permute-start(bf16[144,384]{1,0:T(8,128)(2,1)S(1)} %fusion.4), channel_id=1, source_target_pairs={{0,2},{1,3},{2,0},{3,1},{4,6},{5,7},{6,4},{7,5},{8,10},{9,11},{10,... | collective-permute-start | bytes 331784 | tf_op jit(solution)/shard_map/ppermute | solution.py:269
  118.1 4.8 %collective-permute-start.12 = (bf16[144,384]{1,0:T(8,128)(2,1)S(1)}, bf16[144,384]{1,0:T(8,128)(2,1)S(1)}, u32[]{:S(2)}, u32[]{:S(2)}) collective-permute-start(bf16[144,384]{1,0:T(8,128)(2,1)S(1)} %fusion.7), channel_id=1, source_target_pairs={{0,2},{1,3},{2,0},{3,1},{4,6},{5,7},{6,4},{7,5},{8,10},{9,11},{10,... | collective-permute-start | bytes 331784 | tf_op jit(solution)/shard_map/ppermute | solution.py:269
  119.7 3.4 %collective-permute-start.20 = (bf16[2,144,384]{2,1,0:T(8,128)(2,1)S(1)}, bf16[2,144,384]{2,1,0:T(8,128)(2,1)S(1)}, u32[]{:S(2)}, u32[]{:S(2)}) collective-permute-start(bf16[2,144,384]{2,1,0:T(8,128)(2,1)S(1)} %maximum_select_fusion.5), channel_id=1, source_target_pairs={{0,1},{1,0},{2,3},{3,2},{4,5},{5,4},{6,7},{7,6},{8,9},{9,8},{10,11... | collective-permute-start | bytes 663560 | tf_op jit(solution)/shard_map/ppermute | solution.py:271
  122.9 1.5 %collective-permute-start.13 = (bf16[2,144,384]{2,1,0:T(8,128)(2,1)S(1)}, bf16[2,144,384]{2,1,0:T(8,128)(2,1)S(1)}, u32[]{:S(2)}, u32[]{:S(2)}) collective-permute-start(bf16[2,144,384]{2,1,0:T(8,128)(2,1)S(1)} %maximum_select_fusion.3), channel_id=1, source_target_pairs={{0,1},{1,0},{2,3},{3,2},{4,5},{5,4},{6,7},{7,6},{8,9},{9,8},{10,11... | collective-permute-start | bytes 663560 | tf_op jit(solution)/shard_map/ppermute | solution.py:271
  (20 other events, 75.2 us)

commit v2 on v1

v2 whole, which is shorter than its diff:
```python
import math

import jax
import jax.numpy as jnp
from jax import lax
from jax.experimental import pallas as pl
from jax.experimental.pallas import tpu as pltpu
from jax.sharding import PartitionSpec as P

DILATION_FIRST = 512
DILATION_SECOND = 1024


EPS = 1e-06
SLOPE = math.sqrt(2.0 / math.pi)
CUBIC = 0.044715
F32 = jnp.float32
BF16 = jnp.bfloat16
CUTS = (0, 512, 768)


def shifted(value, axis, steps):
    count = lax.axis_size(axis)
    initial, last = (max(0, -steps), min(count, count - steps))
    return lax.ppermute(value, axis, [(source, source + steps) for source in range(initial, last)])


def gelu_slope(normed):
    inner = jnp.tanh(SLOPE * (normed + CUBIC * normed * normed * normed))
    return 0.5 * (1.0 + inner) + 0.5 * normed * (1.0 - inner * inner) * SLOPE * (
        1.0 + 3.0 * CUBIC * normed * normed
    )


def prepare(inputs, gain_vec):
    xfloat = inputs.astype(F32)
    meansq = jnp.mean(xfloat * xfloat, axis=1, keepdims=True)
    scale = lax.rsqrt(meansq + EPS)
    normed = xfloat * scale * gain_vec[None, :, None]
    gelu_out = jax.nn.gelu(normed, approximate=True).astype(BF16)
    return (xfloat, scale, normed, gelu_out)


def input_grad(xfloat, scale, normed, gain_vec, weight, grad_out, grad_upper, grad_lower):
    dgelu = jnp.einsum("co,sop->scp", weight[0], grad_upper, preferred_element_type=F32)
    dgelu = dgelu + jnp.einsum("co,sop->scp", weight[1], grad_out, preferred_element_type=F32)
    dgelu = dgelu + jnp.einsum("co,sop->scp", weight[2], grad_lower, preferred_element_type=F32)
    dnorm = dgelu * gelu_slope(normed) * gain_vec[None, :, None]
    inner = jnp.mean(dnorm * xfloat, axis=1, keepdims=True)
    dinput = scale * dnorm - xfloat * scale * scale * scale * inner
    return (grad_out.astype(F32) + dinput).astype(BF16)


def general(e_split, u_one, u_two, w_one, w_two, c_one, c_two):
    width = u_one.shape[2]
    factor = 1.0 / math.sqrt(
        u_one.shape[0] * lax.axis_size("batch") * width * lax.axis_size("seq")
    )
    e_two = lax.all_to_all(e_split, "seq", split_axis=2, concat_axis=1, tiled=True)
    span = DILATION_SECOND // width
    lower, upper = shifted(e_two, "seq", span), shifted(e_two, "seq", -span)
    xfloat, scale, normed, _ = prepare(u_two, c_two)
    e_one = input_grad(xfloat, scale, normed, c_two, w_two, e_two, upper, lower)
    span = DILATION_FIRST // width
    lower, upper = shifted(e_one, "seq", span), shifted(e_one, "seq", -span)
    xfloat, scale, normed, gelu_out = prepare(u_one, c_one)
    total = input_grad(xfloat, scale, normed, c_one, w_one, e_one, upper, lower)
    pieces = [
        jnp.einsum("scp,sop->co", gelu_out, tapped, preferred_element_type=F32)
        for tapped in (upper, e_one, lower)
    ]
    terms = jnp.concatenate(pieces, axis=0) * factor
    rows = lax.psum_scatter(terms, "seq", scatter_dimension=0, tiled=True)
    return (total, lax.psum(rows, "batch"))


MIB = 1 << 20


def vmem():
    return pl.BlockSpec(memory_space=pltpu.VMEM)


def scalars():
    return pl.BlockSpec(memory_space=pltpu.SMEM)


def cut(e_split, place, width):
    part = e_split.shape[0]
    peers = (3, 2, 1, 0)

    def body(place_ref, e_ref, *rest):
        outs, sems = rest[:4], rest[4]
        me = place_ref[0]
        copies = []
        for n, k in enumerate(peers):
            for j in range(2):
                at = pl.multiple_of((me ^ k ^ (2 * j)) * width, width)
                copies.append(
                    pltpu.make_async_copy(
                        e_ref.at[:, pl.ds(at, width)], outs[n].at[j], sems.at[2 * n + j]
                    )
                )
        for copy in copies:
            copy.start()
        for copy in copies:
            copy.wait()

    return pl.pallas_call(
        body,
        in_specs=[scalars(), pl.BlockSpec(memory_space=pltpu.HBM)],
        out_specs=[vmem()] * 4,
        out_shape=[pltpu.VMEM((2, part, width), BF16)] * 4,
        scratch_shapes=[pltpu.SemaphoreType.DMA((8,))],
        cost_estimate=pl.CostEstimate(
            flops=0, bytes_accessed=32 * part * width, transcendentals=0
        ),
        compiler_params=pltpu.CompilerParams(vmem_limit_bytes=4 * MIB),
        name="cut",
    )(place, e_split)


def prep(u_two, c_two, u_one, c_one):
    chans, width = u_one.shape
    tile = 128
    wide, row = pltpu.VMEM((chans, width), F32), pltpu.VMEM((1, width), F32)
    copy = pltpu.VMEM((chans, width), BF16)

    def layer(u_ref, c_ref, q_ref, r_ref, v_ref, g_ref):
        c = c_ref[...]
        for t in range(width // tile):
            cols = slice(t * tile, (t + 1) * tile)
            v_ref[:, cols] = u_ref[:, cols]
            u = u_ref[:, cols].astype(F32)
            r = lax.rsqrt(jnp.mean(u * u, axis=0, keepdims=True) + EPS)
            a = u * r * c
            inner = jnp.tanh(SLOPE * (a + CUBIC * a * a * a))
            slope = 0.5 * (1.0 + inner) + 0.5 * a * (1.0 - inner * inner) * SLOPE * (
                1.0 + 3.0 * CUBIC * a * a
            )
            q_ref[:, cols] = slope * c
            r_ref[:, cols] = r
            if g_ref is not None:
                g_ref[:, cols] = (0.5 * a * (1.0 + inner)).astype(BF16)

    def body(u2, c2, u1, c1, q2, r2, v2, q1, r1, v1, g1):
        layer(u2, c2, q2, r2, v2, None)
        layer(u1, c1, q1, r1, v1, g1)

    return pl.pallas_call(
        body,
        in_specs=[vmem()] * 4,
        out_specs=[vmem()] * 7,
        out_shape=[wide, row, copy, wide, row, copy, copy],
        cost_estimate=pl.CostEstimate(
            flops=60 * chans * width,
            bytes_accessed=16 * chans * width,
            transcendentals=2 * chans * width,
        ),
        compiler_params=pltpu.CompilerParams(vmem_limit_bytes=8 * MIB),
        name="prep",
    )(u_two, c_two.reshape(chans, 1), u_one, c_one.reshape(chans, 1))


def finish(acc, e, u, q, r):
    dn = acc * q
    mean = jnp.mean(dn * u, axis=0, keepdims=True)
    return e + r * dn - u * (r * r * r * mean)


def middle(pieces, w, u, q, r, place, cuts):
    chans, width = u.shape
    part = pieces[0].shape[1]
    chunks = len(cuts) - 1
    tile = 256

    def body(place_ref, p0, p1, p2, p3, w_ref, u_ref, q_ref, r_ref, *rest):
        outs, e_s = rest[:chunks], rest[chunks]
        me = place_ref[0]
        tap = place_ref[1]
        for k, piece in enumerate((p0, p1, p2, p3)):
            at = pl.multiple_of((me ^ k) * part, part)
            for j in range(2):
                e_s[j, pl.ds(at, part), :] = piece[j]
        for t in range(width // tile):
            cols = slice(t * tile, (t + 1) * tile)
            e = e_s[0, :, cols]
            acc = jnp.dot(w_ref[1], e, preferred_element_type=F32)
            acc = acc + jnp.dot(w_ref[tap], e_s[1, :, cols], preferred_element_type=F32)
            out = finish(
                acc, e.astype(F32), u_ref[:, cols].astype(F32), q_ref[:, cols], r_ref[:, cols]
            ).astype(BF16)
            for n in range(chunks):
                outs[n][:, cols] = out[cuts[n] : cuts[n + 1]]

    return pl.pallas_call(
        body,
        in_specs=[scalars()] + [vmem()] * 8,
        out_specs=[vmem()] * chunks,
        out_shape=[pltpu.VMEM((b - a, width), BF16) for a, b in zip(cuts, cuts[1:])],
        scratch_shapes=[pltpu.VMEM((2, chans, width), BF16)],
        cost_estimate=pl.CostEstimate(
            flops=4 * chans * chans * width, bytes_accessed=10 * chans * width, transcendentals=0
        ),
        compiler_params=pltpu.CompilerParams(vmem_limit_bytes=10 * MIB),
        name="middle",
    )(place, *pieces, w, u, q, r)


def segments(tap, chans, block):
    cuts, row = [], tap * chans
    while row < (tap + 1) * chans:
        end = min((row // block + 1) * block, (tap + 1) * chans)
        cuts.append((row - tap * chans, end - row))
        row = end
    return cuts


def taps(g, own, near, far, place, factor, seq):
    chans, width = g.shape
    block = 3 * chans // seq
    outer = own is None
    sources = [near, far] if outer else list(own)
    sizes = [source.shape[0] for source in sources]
    cols = sizes[0] if outer else sum(sizes)
    kinds = (0, 2) if outer else (1,)
    rows = chans // 4

    def body(place_ref, g_ref, *refs):
        e_refs, (keep_ref, send_ref, acc_s, sem) = refs[:2], refs[2:]
        core = place_ref[2]
        g_all = g_ref[...]
        if outer:
            even = place_ref[3] == 0
            a, b = e_refs[0][...], e_refs[1][...]
            jobs = [(0, 0, 0, jnp.where(even, a, b)), (1, 2, 0, jnp.where(even, b, a))]
        else:
            jobs = [(0, 1, sum(sizes[:n]), ref[...]) for n, ref in enumerate(e_refs)]
        for slot, tap, col, e in jobs:
            acc = lax.dot_general(
                g_all, e, (((1,), (1,)), ((), ())), preferred_element_type=F32
            )
            acc = acc * factor
            base = slot * rows
            for start, length in segments(tap, chans, block):
                part = length // 4
                for q in range(4):
                    row = start + q * part
                    acc_s[q // 2, q % 2, base : base + part, col : col + e.shape[0]] = acc[
                        row : row + part
                    ]
                base += part
        copy = pltpu.make_async_copy(acc_s.at[core], keep_ref, sem)
        copy.start()
        send_ref[...] = acc_s[1 - core].astype(BF16)
        copy.wait()

    shape = (2, rows * len(kinds), cols)
    return pl.pallas_call(
        body,
        in_specs=[scalars()] + [vmem()] * 3,
        out_specs=[vmem(), vmem()],
        out_shape=[pltpu.VMEM(shape, F32), pltpu.VMEM(shape, BF16)],
        scratch_shapes=[pltpu.VMEM((2,) + shape, F32), pltpu.SemaphoreType.DMA],
        cost_estimate=pl.CostEstimate(
            flops=2 * len(kinds) * chans * cols * width,
            bytes_accessed=4 * len(kinds) * chans * cols,
            transcendentals=0,
        ),
        compiler_params=pltpu.CompilerParams(vmem_limit_bytes=14 * MIB),
    )(place, g, *sources)


def assemble(chunks, place):
    rows = chunks[0][0].shape[0]
    cuts = [0]
    for chunk in chunks:
        cuts.append(cuts[-1] + chunk[0].shape[1])
    grain = 48
    grains = rows // grain

    def body(place_ref, *refs):
        out_ref = refs[-1]
        core, x, first = place_ref[2], place_ref[4], place_ref[5]
        for n in range(len(chunks)):
            for k, ref in enumerate(refs[4 * n : 4 * n + 4]):
                q = 2 * (core ^ (k // 2)) + (x ^ (k % 2))
                for j in range(grains):
                    dest = jnp.where(
                        j < first, first * q + j, 4 * first + (grains - first) * q + j - first
                    )
                    at = pl.multiple_of(dest * grain, grain)
                    out_ref[pl.ds(at, grain), cuts[n] : cuts[n + 1]] = ref[
                        j * grain : (j + 1) * grain
                    ].astype(F32)

    return pl.pallas_call(
        body,
        in_specs=[scalars()] + [vmem()] * (4 * len(chunks)),
        out_specs=vmem(),
        out_shape=jax.ShapeDtypeStruct((4 * rows, cuts[-1]), F32),
        compiler_params=pltpu.CompilerParams(vmem_limit_bytes=8 * MIB),
        name="assemble",
    )(place, *[value for chunk in chunks for value in chunk])


def last(owns, nears, fars, w, u, q, r, place):
    chans, width = u.shape
    chunks = len(owns)
    tile = 256

    def body(place_ref, *refs):
        e_refs = refs[: 3 * chunks]
        w_ref, u_ref, q_ref, r_ref, out_ref = refs[3 * chunks :]
        tap = 2 * place_ref[3]
        for t in range(width // tile):
            cols = slice(t * tile, (t + 1) * tile)
            acc = jnp.zeros((chans, tile), F32)
            for n, k in enumerate((1, tap, 2 - tap)):
                e = jnp.concatenate(
                    [ref[:, cols] for ref in e_refs[n * chunks : (n + 1) * chunks]], axis=0
                )
                if n == 0:
                    own = e.astype(F32)
                acc = acc + jnp.dot(w_ref[k], e, preferred_element_type=F32)
            out_ref[:, cols] = finish(
                acc, own, u_ref[:, cols].astype(F32), q_ref[:, cols], r_ref[:, cols]
            ).astype(BF16)

    return pl.pallas_call(
        body,
        in_specs=[scalars()] + [vmem()] * (3 * chunks + 4),
        out_specs=vmem(),
        out_shape=jax.ShapeDtypeStruct((chans, width), BF16),
        cost_estimate=pl.CostEstimate(
            flops=6 * chans * chans * width, bytes_accessed=12 * chans * width, transcendentals=0
        ),
        compiler_params=pltpu.CompilerParams(vmem_limit_bytes=10 * MIB),
        name="last",
    )(place, *owns, *nears, *fars, w, u, q, r)


def glue(body, outs, *args):
    moved_bytes = sum(a.size * a.dtype.itemsize for a in args)
    return pl.pallas_call(
        body,
        in_specs=[scalars()] + [vmem()] * (len(args) - 1),
        out_specs=[vmem()] * len(outs),
        out_shape=[pltpu.VMEM(*out) for out in outs],
        cost_estimate=pl.CostEstimate(flops=0, bytes_accessed=moved_bytes, transcendentals=0),
        compiler_params=pltpu.CompilerParams(vmem_limit_bytes=4 * MIB),
    )(*args)


def after_core(keep, far, place):
    shape = keep.shape[1:]

    def body(place_ref, keep_ref, far_ref, own_ref, send_ref):
        x = place_ref[4]
        own_ref[...] = keep_ref[x] + far_ref[x].astype(F32)
        send_ref[...] = (keep_ref[1 - x] + far_ref[1 - x].astype(F32)).astype(BF16)

    return glue(body, [(shape, F32), (shape, BF16)], place, keep, far)


def after_x(outer, far, center, far_center, columns, seq, place):
    rows, cols = outer.shape
    third = rows // 2
    unit = 3 * third // seq

    def body(place_ref, a_ref, fa_ref, b_ref, fb_ref, keep_ref, send_ref, part_s):
        me = place_ref[0]
        for tap in range(3):
            if tap == 1:
                value = b_ref[:, columns] + fb_ref[:, columns].astype(F32)
            else:
                at = slice(tap // 2 * third, (tap // 2 + 1) * third)
                value = a_ref[at] + fa_ref[at].astype(F32)
            row = tap * third
            while row < (tap + 1) * third:
                end = min((row // unit + 1) * unit, (tap + 1) * third)
                base = row // unit * unit
                part_s[row // unit, row - base : end - base] = value[
                    row - tap * third : end - tap * third
                ]
                row = end
        for n in range(2):
            keep_ref[n] = part_s[me ^ (2 * n)]
            send_ref[n] = part_s[me ^ (2 * n + 1)].astype(BF16)

    shape = (2, unit, cols)
    args = (place, outer, far, center, far_center)
    return pl.pallas_call(
        body,
        in_specs=[scalars()] + [vmem()] * 4,
        out_specs=[vmem()] * 2,
        out_shape=[pltpu.VMEM(shape, F32), pltpu.VMEM(shape, BF16)],
        scratch_shapes=[pltpu.VMEM((seq, unit, cols), F32)],
        cost_estimate=pl.CostEstimate(
            flops=0, bytes_accessed=12 * seq * unit * cols, transcendentals=0
        ),
        compiler_params=pltpu.CompilerParams(vmem_limit_bytes=6 * MIB),
    )(*args)


def after_near(keep, near, place):
    shape = keep.shape[1:]

    def body(place_ref, keep_ref, near_ref, own_ref, send_ref):
        own_ref[...] = keep_ref[0] + near_ref[0].astype(F32)
        send_ref[...] = (keep_ref[1] + near_ref[1].astype(F32)).astype(BF16)

    return glue(body, [(shape, F32), (shape, BF16)], place, keep, near)


def after_far(own, far, place):
    def body(place_ref, own_ref, far_ref, out_ref):
        out_ref[...] = (own_ref[...] + far_ref[...].astype(F32)).astype(BF16)

    return glue(body, [(own.shape, BF16)], place, own, far)[0]


def pairs(count, flip):
    return [(i, i ^ flip) for i in range(count)]


def four_shards(e_split, u_one, u_two, w_one, w_two, c_one, c_two):
    seq, batch = lax.axis_size("seq"), lax.axis_size("batch")
    me = lax.axis_index("seq")
    core, x = lax.axis_index("batch") % 2, lax.axis_index("batch") // 2
    e_split, u_one, u_two = e_split[0], u_one[0], u_two[0]
    chans, width = u_one.shape
    factor = 1.0 / math.sqrt(batch * width * seq)
    block = 3 * chans // seq
    first = jnp.minimum(block, chans - (block * me) % chans) // (4 * 48)
    place = jnp.stack([me, jnp.where(me < 2, 0, 2), core, me % 2, x, first]).astype(jnp.int32)

    three, two, one, own = cut(e_split, place, width)
    three = lax.ppermute(three, "seq", pairs(seq, 3))
    two = lax.ppermute(two, "seq", pairs(seq, 2))
    one = lax.ppermute(one, "seq", pairs(seq, 1))
    q_two, r_two, v_two, q_one, r_one, v_one, g_one = prep(u_two, c_two, u_one, c_one)
    owns = middle((own, one, two, three), w_two, v_two, q_two, r_two, place, CUTS)
    nears = [lax.ppermute(e, "seq", pairs(seq, 1)) for e in owns]
    fars = [lax.ppermute(e, "seq", [(1, 2), (2, 1)]) for e in owns]

    def over_batch(own, near, far):
        keep, send = taps(g_one, own, near, far, place, factor, seq)
        send = lax.ppermute(send, "batch", pairs(batch, 1))
        keep, send = after_core(keep, send, place)
        return keep, lax.ppermute(send, "batch", pairs(batch, 2))

    center = over_batch(owns, None, None)
    chunks = []
    for j in range(len(owns)):
        outer = over_batch(None, nears[j], fars[j])
        columns = slice(CUTS[j], CUTS[j + 1])
        keep, send = after_x(*outer, *center, columns, seq, place)
        near = lax.ppermute(send, "seq", pairs(seq, 1))
        keep, send = after_near(keep, near, place)
        far = lax.ppermute(send, "seq", pairs(seq, 2))
        mine = after_far(keep, far, place)
        over_x = lax.ppermute(mine, "batch", pairs(batch, 2))
        over_core = lax.ppermute(mine, "batch", pairs(batch, 1))
        over_both = lax.ppermute(over_x, "batch", pairs(batch, 1))
        chunks.append((mine, over_x, over_core, over_both))
    gradient = assemble(chunks, place)
    total = last(owns, nears, fars, w_one, v_one, q_one, r_one, place)
    return (total[None], gradient)


def fits(sizes, width, samples):
    return (
        sizes["seq"] == 4
        and sizes["batch"] == 4
        and width == DILATION_FIRST
        and 2 * width == DILATION_SECOND
        and samples == 1
    )


def on_device(e_split, u_one, u_two, *rest):
    sizes = {name: lax.axis_size(name) for name in ("seq", "batch")}
    if not fits(sizes, u_one.shape[2], u_one.shape[0]):
        return general(e_split, u_one, u_two, *rest)
    return four_shards(e_split, u_one, u_two, *rest)


def solution(mesh):
    in_specs = (
        P(("grp", "batch"), "seq", None),
        P(("grp", "batch"), None, "seq"),
        P(("grp", "batch"), None, "seq"),
        P(),
        P(),
        P(),
        P(),
    )
    out_specs = (P(("grp", "batch"), None, "seq"), P(("grp", "seq"), None))
    return jax.shard_map(
        on_device, mesh=mesh, in_specs=in_specs, out_specs=out_specs, check_vma=False
    )
```

time: 127 us -> 121 us (0.953)
  waiting for transfers between devices: 42.2 us -> 53.5 us
  other arithmetic: 7.44 us -> 0 us
  local copies, waits for them, and re-layouts: 10 us -> 5.18 us
  starting transfers between devices: 39.6 us -> 36.4 us
    ppermute x21 -> x23, waiting for transfers between devices: 42.2 us -> 53.5 us  [the longest x2 14.5 us: four_shards(): nears = [lax.ppermute(e, 'seq', pairs(seq, 1)) for e in owns]]
    ppermute x21 -> x23, starting transfers between devices: 39.6 us -> 36.4 us  [the longest x2 14 us: four_shards(): nears = [lax.ppermute(e, 'seq', pairs(seq, 1)) for e in owns]]
    add x4 -> x0, other arithmetic: 3.08 us -> none  [the longest x2 2.92 us: reduced(): part = keep + lax.ppermute(send, 'batch', pairs(batch, 1)).astype(F32)]
    unnamed x46 -> x10, local copies, waits for them, and re-layouts: 6.44 us -> 3.41 us
    another operation x4 -> x0, other arithmetic: 2.61 us -> none  [the longest x3 2.53 us: four_shards(): pieces = [jnp.stack([block(me ^ k), block(me ^ k ^ 2)]) for k in range(4)]]
    dynamic_slice x1 -> x0, local copies, waits for them, and re-layouts: 1.53 us -> none  [block(): return lax.dynamic_slice(e_split, (0, index * width), (part, width))]
    concatenate x1 -> x0, other arithmetic: 1.33 us -> none  [four_shards(): return (total[None], jnp.concatenate(chunks, axis=1))]
    pallas_call x6 -> x17, Pallas kernels: 25.5 us -> 24.4 us  [the longest x1 4.87 us: prep(): pl.pallas_call(body, in_specs=[vmem()] * 4, out_specs=[vmem()] * 7, out_s...]
  transfers between devices with their start and end apart: 21 -> 23, of which waited for: 10 -> 9; matrix products, arithmetic and copies ran while one was open for 6% -> 1% of each run, Pallas kernels for 16% -> 14%
where the time goes in v2:
time: 121 us; the launch traced here: 120 us
  waiting for transfers between devices  53.5 us (44%)
  starting transfers between devices  36.4 us (30%)
  Pallas kernels  24.4 us (20%)
  local copies, waits for them, and re-layouts  5.18 us (4%)
    ppermute x2, waiting for transfers between devices, four_shards(): nears = [lax.ppermute(e, 'seq', pairs(seq, 1)) for e in owns]  14.5 us
    ppermute x2, starting transfers between devices, four_shards(): nears = [lax.ppermute(e, 'seq', pairs(seq, 1)) for e in owns]  14 us
    ppermute x1, waiting for transfers between devices, four_shards(): two = lax.ppermute(two, 'seq', pairs(seq, 2))  12.9 us
    ppermute x3, waiting for transfers between devices, over_batch(): return (keep, lax.ppermute(send, 'batch', pairs(batch, 2)))  12.6 us
    ppermute x1, waiting for transfers between devices, four_shards(): one = lax.ppermute(one, 'seq', pairs(seq, 1))  5.36 us
    pallas_call x1, Pallas kernels, prep(): pl.pallas_call(body, in_specs=[vmem()] * 4, out_specs=[vmem()] * 7, out_s...  4.87 us
    pallas_call x3, Pallas kernels, taps(): pl.pallas_call(body, in_specs=[scalars()] + [vmem()] * 3, out_specs=[vmem...  4.73 us
    ppermute x3, starting transfers between devices, over_batch(): return (keep, lax.ppermute(send, 'batch', pairs(batch, 2)))  4.64 us
  transfers between devices with their start and end apart: 23, of which 9 were waited for; matrix products, arithmetic and copies ran while one was open for 1% of the time, Pallas kernels for 14%

profile of v2, /device:TPU:0, one launch (start us, length us, event | category | flops | bytes accessed | tf_op | source)
XLA Modules:
  0.0 120.3 jit_solution(2673919096018988192)
XLA Ops:
  2.8 3.1 %collective-permute-start = (bf16[2,192,512]{2,1,0:T(8,128)(2,1)S(1)}, bf16[2,192,512]{2,1,0:T(8,128)(2,1)S(1)}, u32[]{:S(2)}, u32[]{:S(2)}) collective-permute-start(bf16[2,192,512]{2,1,0:T(8,128)(2,1)S(1)} %get-tuple-element.36), channel_id=1, source_target_pairs={{0,4},{4,0},{8,12},{12,8},{1,5},{5,1},{9,13},{13,9},{2,6},{6,2},{1... | collective-permute-start | bytes 1179656 | tf_op jit(solution)/shard_map/ppermute | solution.py:441
  5.9 2.6 %collective-permute-start.1 = (bf16[2,192,512]{2,1,0:T(8,128)(2,1)S(1)}, bf16[2,192,512]{2,1,0:T(8,128)(2,1)S(1)}, u32[]{:S(2)}, u32[]{:S(2)}) collective-permute-start(bf16[2,192,512]{2,1,0:T(8,128)(2,1)S(1)} %get-tuple-element.37), channel_id=1, source_target_pairs={{0,8},{4,12},{8,0},{12,4},{1,9},{5,13},{9,1},{13,5},{2,10},{6,14},... | collective-permute-start | bytes 1179656 | tf_op jit(solution)/shard_map/ppermute | solution.py:440
  12.5 4.9 %prep.1 = (f32[768,512]{1,0:T(8,128)S(1)}, f32[1,512]{1,0:T(1,128)S(1)}, bf16[768,512]{1,0:T(8,128)(2,1)S(1)}, f32[768,512]{1,0:T(8,128)S(1)}, f32[1,512]{1,0:T(...) custom-call(bf16[768,512]{1,0:T(8,128)(2,1)S(1)} %bitcast.11, f32[768,1]{1,0:T(8,128)S(1)} %reshape.12.c2, ...), custom_call_target="tpu_custom_call" | custom-call | flops 23592960 | bytes 6291456 | tf_op jit(solution)/shard_map/prep/pallas_call | solution.py:150
  17.3 5.4 %collective-permute-done.p1 = bf16[2,192,512]{2,1,0:T(8,128)(2,1)S(1)} collective-permute-done((bf16[2,192,512]{2,1,0:T(8,128)(2,1)S(1)}, bf16[2,192,512]{2,1,0:T(8,128)(2,1)S(1)}, u32[]{:S(2)}, u32[]{:S(2)}) %collective-permute-start) | collective-permute-done | bytes 393248 | tf_op jit(solution)/shard_map/ppermute | solution.py:441
  22.7 12.9 %collective-permute-done.1.p2 = bf16[2,192,512]{2,1,0:T(8,128)(2,1)S(1)} collective-permute-done((bf16[2,192,512]{2,1,0:T(8,128)(2,1)S(1)}, bf16[2,192,512]{2,1,0:T(8,128)(2,1)S(1)}, u32[]{:S(2)}, u32[]{:S(2)}) %collective-permute-start.1) | collective-permute-done | bytes 393248 | tf_op jit(solution)/shard_map/ppermute | solution.py:440
  35.6 2.5 %middle.1 = (bf16[512,512]{1,0:T(8,128)(2,1)S(1)}, bf16[256,512]{1,0:T(8,128)(2,1)S(1)}) custom-call(s32[6]{0:T(128)S(1)} %stack.27.place_ref, bf16[2,192,512]{2,1,0:T(8,128)(2,1)S(1)} %get-tuple-element.35.p0, bf16[2,192,512]{2,1,0:T(8,128)(2,1)S(1)} %collective-permute-done.p1, bf16[2,192,512]{2,1,0:T(8,128)(2,1)S(1)} %collective-permute-done.1.p2, ...), custom_call_target="tpu_custom_call" | custom-call | flops 1207959552 | bytes 3932160 | tf_op jit(solution)/shard_map/middle/pallas_call | solution.py:196
  38.9 10.5 %collective-permute-start.3 = (bf16[512,512]{1,0:T(8,128)(2,1)S(1)}, bf16[512,512]{1,0:T(8,128)(2,1)S(1)}, u32[]{:S(2)}, u32[]{:S(2)}) collective-permute-start(bf16[512,512]{1,0:T(8,128)(2,1)S(1)} %get-tuple-element.42.refs_0_), channel_id=1, source_target_pairs={{0,4},{4,0},{8,12},{12,8},{1,5},{5,1},{9,13},{13,9},{2,6},{6,2},{1... | collective-permute-start | bytes 1572872 | tf_op jit(solution)/shard_map/ppermute | solution.py:444
  49.4 10.5 %collective-permute-done.3.refs_2_.refs_0_ = bf16[512,512]{1,0:T(8,128)(2,1)S(1)} collective-permute-done((bf16[512,512]{1,0:T(8,128)(2,1)S(1)}, bf16[512,512]{1,0:T(8,128)(2,1)S(1)}, u32[]{:S(2)}, u32[]{:S(2)}) %collective-permute-start.3) | collective-permute-done | bytes 524320 | tf_op jit(solution)/shard_map/ppermute | solution.py:444
  59.9 1.8 %shard_map.86 = (f32[2,384,512]{2,1,0:T(8,128)S(1)}, bf16[2,384,512]{2,1,0:T(8,128)(2,1)S(1)}) custom-call(s32[6]{0:T(128)S(1)} %stack.27.place_ref, bf16[768,512]{1,0:T(8,128)(2,1)S(1)} %get-tuple-element.47.g_ref, bf16[512,512]{1,0:T(8,128)(2,1)S(1)} %collective-permute-done.3.refs_2_.refs_0_, bf16[512,512]{1,0:T(8,128)(2,1)S(1)} %collective-permute-done.5.refs_4_.refs_1_), custom_call_target="tpu_custom_call" | custom-call | flops 805306368 | bytes 3145728 | tf_op jit(solution)/shard_map/pallas_call | solution.py:259
  61.8 1.7 %shard_map.88 = (f32[2,192,768]{2,1,0:T(8,128)S(1)}, bf16[2,192,768]{2,1,0:T(8,128)(2,1)S(1)}) custom-call(s32[6]{0:T(128)S(1)} %stack.27.place_ref, bf16[768,512]{1,0:T(8,128)(2,1)S(1)} %get-tuple-element.47.g_ref, bf16[512,512]{1,0:T(8,128)(2,1)S(1)} %get-tuple-element.42.refs_0_, bf16[256,512]{1,0:T(8,128)(2,1)S(1)} %get-tuple-element.43.refs_1_), custom_call_target="tpu_custom_call" | custom-call | flops 603979776 | bytes 2359296 | tf_op jit(solution)/shard_map/pallas_call | solution.py:259
  64.9 3.5 %collective-permute-start.4 = (bf16[256,512]{1,0:T(8,128)(2,1)S(1)}, bf16[256,512]{1,0:T(8,128)(2,1)S(1)}, u32[]{:S(2)}, u32[]{:S(2)}) collective-permute-start(bf16[256,512]{1,0:T(8,128)(2,1)S(1)} %get-tuple-element.43.refs_1_), channel_id=1, source_target_pairs={{0,4},{4,0},{8,12},{12,8},{1,5},{5,1},{9,13},{13,9},{2,6},{6,2},{1... | collective-permute-start | bytes 786440 | tf_op jit(solution)/shard_map/ppermute | solution.py:444
  69.1 1.5 %collective-permute-start.8 = (bf16[384,512]{1,0:T(8,128)(2,1)S(1)}, bf16[384,512]{1,0:T(8,128)(2,1)S(1)}, u32[]{:S(2)}, u32[]{:S(2)}) collective-permute-start(bf16[384,512]{1,0:T(8,128)(2,1)S(1)} %get-tuple-element.51), channel_id=1, source_target_pairs={{0,2},{1,3},{2,0},{3,1},{4,6},{5,7},{6,4},{7,5},{8,10},{9,11},{10,... | collective-permute-start | bytes 1179656 | tf_op jit(solution)/shard_map/ppermute | solution.py:451
  70.6 4.0 %collective-permute-done.4.refs_3_.refs_0_ = bf16[256,512]{1,0:T(8,128)(2,1)S(1)} collective-permute-done((bf16[256,512]{1,0:T(8,128)(2,1)S(1)}, bf16[256,512]{1,0:T(8,128)(2,1)S(1)}, u32[]{:S(2)}, u32[]{:S(2)}) %collective-permute-start.4) | collective-permute-done | bytes 262176 | tf_op jit(solution)/shard_map/ppermute | solution.py:444
  78.2 7.9 %collective-permute-done.10.fb_ref = bf16[192,768]{1,0:T(8,128)(2,1)S(1)} collective-permute-done((bf16[192,768]{1,0:T(8,128)(2,1)S(1)}, bf16[192,768]{1,0:T(8,128)(2,1)S(1)}, u32[]{:S(2)}, u32[]{:S(2)}) %collective-permute-start.10) | collective-permute-done | bytes 294944 | tf_op jit(solution)/shard_map/ppermute | solution.py:451
  86.8 1.8 %collective-permute-start.11 = (bf16[2,144,512]{2,1,0:T(8,128)(2,1)S(1)}, bf16[2,144,512]{2,1,0:T(8,128)(2,1)S(1)}, u32[]{:S(2)}, u32[]{:S(2)}) collective-permute-start(bf16[2,144,512]{2,1,0:T(8,128)(2,1)S(1)} %get-tuple-element.57), channel_id=1, source_target_pairs={{0,4},{4,0},{8,12},{12,8},{1,5},{5,1},{9,13},{13,9},{2,6},{6,2},{1... | collective-permute-start | bytes 884744 | tf_op jit(solution)/shard_map/ppermute | solution.py:459
  89.3 1.5 %collective-permute-start.17 = (bf16[384,256]{1,0:T(8,128)(2,1)S(1)}, bf16[384,256]{1,0:T(8,128)(2,1)S(1)}, u32[]{:S(2)}, u32[]{:S(2)}) collective-permute-start(bf16[384,256]{1,0:T(8,128)(2,1)S(1)} %get-tuple-element.63), channel_id=1, source_target_pairs={{0,2},{1,3},{2,0},{3,1},{4,6},{5,7},{6,4},{7,5},{8,10},{9,11},{10,... | collective-permute-start | bytes 589832 | tf_op jit(solution)/shard_map/ppermute | solution.py:451
  90.8 4.7 %collective-permute-done.17.fa_ref = bf16[384,256]{1,0:T(8,128)(2,1)S(1)} collective-permute-done((bf16[384,256]{1,0:T(8,128)(2,1)S(1)}, bf16[384,256]{1,0:T(8,128)(2,1)S(1)}, u32[]{:S(2)}, u32[]{:S(2)}) %collective-permute-start.17) | collective-permute-done | bytes 196640 | tf_op jit(solution)/shard_map/ppermute | solution.py:451
  97.1 2.8 %collective-permute-start.12 = (bf16[144,512]{1,0:T(8,128)(2,1)S(1)}, bf16[144,512]{1,0:T(8,128)(2,1)S(1)}, u32[]{:S(2)}, u32[]{:S(2)}) collective-permute-start(bf16[144,512]{1,0:T(8,128)(2,1)S(1)} %get-tuple-element.59), channel_id=1, source_target_pairs={{0,8},{4,12},{8,0},{12,4},{1,9},{5,13},{9,1},{13,5},{2,10},{6,14},... | collective-permute-start | bytes 442376 | tf_op jit(solution)/shard_map/ppermute | solution.py:461
  99.9 2.7 %collective-permute-done.18.near_ref = bf16[2,144,256]{2,1,0:T(8,128)(2,1)S(1)} collective-permute-done((bf16[2,144,256]{2,1,0:T(8,128)(2,1)S(1)}, bf16[2,144,256]{2,1,0:T(8,128)(2,1)S(1)}, u32[]{:S(2)}, u32[]{:S(2)}) %collective-permute-start.18) | collective-permute-done | bytes 147488 | tf_op jit(solution)/shard_map/ppermute | solution.py:459
  103.2 1.7 %collective-permute-start.19 = (bf16[144,256]{1,0:T(8,128)(2,1)S(1)}, bf16[144,256]{1,0:T(8,128)(2,1)S(1)}, u32[]{:S(2)}, u32[]{:S(2)}) collective-permute-start(bf16[144,256]{1,0:T(8,128)(2,1)S(1)} %get-tuple-element.67), channel_id=1, source_target_pairs={{0,8},{4,12},{8,0},{12,4},{1,9},{5,13},{9,1},{13,5},{2,10},{6,14},... | collective-permute-start | bytes 221192 | tf_op jit(solution)/shard_map/ppermute | solution.py:461
  104.8 2.1 %collective-permute-done.12.far_ref = bf16[144,512]{1,0:T(8,128)(2,1)S(1)} collective-permute-done((bf16[144,512]{1,0:T(8,128)(2,1)S(1)}, bf16[144,512]{1,0:T(8,128)(2,1)S(1)}, u32[]{:S(2)}, u32[]{:S(2)}) %collective-permute-start.12) | collective-permute-done | bytes 147488 | tf_op jit(solution)/shard_map/ppermute | solution.py:461
  110.8 3.2 %collective-permute-done.20.refs_5_ = bf16[144,256]{1,0:T(8,128)(2,1)S(1)} collective-permute-done((bf16[144,256]{1,0:T(8,128)(2,1)S(1)}, bf16[144,256]{1,0:T(8,128)(2,1)S(1)}, u32[]{:S(2)}, u32[]{:S(2)}) %collective-permute-start.20) | collective-permute-done | bytes 73760 | tf_op jit(solution)/shard_map/ppermute | solution.py:463
  114.5 3.9 %last.1 = bf16[768,512]{1,0:T(8,128)(2,1)} custom-call(s32[6]{0:T(128)S(1)} %stack.27.place_ref, bf16[512,512]{1,0:T(8,128)(2,1)S(1)} %get-tuple-element.42.refs_0_, bf16[256,512]{1,0:T(8,128)(2,1)S(1)} %get-tuple-element.43.refs_1_, bf16[512,512]{1,0:T(8,128)(2,1)S(1)} %collective-permute-done.3.refs_2_.refs_0_, ...), custom_call_target="tpu_custom_call" | custom-call | flops 1811939328 | bytes 4718592 | tf_op jit(solution)/shard_map/last/pallas_call | solution.py:330
  118.5 1.9 %assemble.1 = f32[576,768]{1,0:T(8,128)} custom-call(s32[6]{0:T(128)S(1)} %stack.27.place_ref, bf16[144,512]{1,0:T(8,128)(2,1)S(1)} %shard_map.92.refs_0_, bf16[144,512]{1,0:T(8,128)(2,1)S(1)} %collective-permute-done.13.refs_1_, bf16[144,512]{1,0:T(8,128)(2,1)S(1)} %collective-permute-done.14.refs_2_, bf16[144,512]{1,0:T(8,128)(2,1)S(1)} %collective-permute-done.15.refs_3_, ...), custom_call_target="tpu_custom_call" | custom-call | tf_op jit(solution)/shard_map/assemble/pallas_call | solution.py:297
  (52 shorter events, 20.3 us)
Async XLA Ops:
  1.9 33.7 %copy-start.1 = (bf16[3,768,768]{2,1,0:T(8,128)(2,1)S(1)}, bf16[3,768,768]{2,1,0:T(8,128)(2,1)}, u32[]{:S(2)}) copy-start(bf16[3,768,768]{2,1,0:T(8,128)(2,1)} %w_ref.1) | copy-start | bytes 10616836
  2.8 19.9 %collective-permute-start = (bf16[2,192,512]{2,1,0:T(8,128)(2,1)S(1)}, bf16[2,192,512]{2,1,0:T(8,128)(2,1)S(1)}, u32[]{:S(2)}, u32[]{:S(2)}) collective-permute-start(bf16[2,192,512]{2,1,0:T(8,128)(2,1)S(1)} %get-tuple-element.36), channel_id=1, source_target_pairs={{0,4},{4,0},{8,12},{12,8},{1,5},{5,1},{9,13},{13,9},{2,6},{6,2},{1... | collective-permute-start | bytes 1179656 | tf_op jit(solution)/shard_map/ppermute | solution.py:441
  5.9 29.7 %collective-permute-start.1 = (bf16[2,192,512]{2,1,0:T(8,128)(2,1)S(1)}, bf16[2,192,512]{2,1,0:T(8,128)(2,1)S(1)}, u32[]{:S(2)}, u32[]{:S(2)}) collective-permute-start(bf16[2,192,512]{2,1,0:T(8,128)(2,1)S(1)} %get-tuple-element.37), channel_id=1, source_target_pairs={{0,8},{4,12},{8,0},{12,4},{1,9},{5,13},{9,1},{13,5},{2,10},{6,14},... | collective-permute-start | bytes 1179656 | tf_op jit(solution)/shard_map/ppermute | solution.py:440
  8.5 27.2 %collective-permute-start.2 = (bf16[2,192,512]{2,1,0:T(8,128)(2,1)S(1)}, bf16[2,192,512]{2,1,0:T(8,128)(2,1)S(1)}, u32[]{:S(2)}, u32[]{:S(2)}) collective-permute-start(bf16[2,192,512]{2,1,0:T(8,128)(2,1)S(1)} %get-tuple-element.38), channel_id=1, source_target_pairs={{0,12},{4,8},{8,4},{12,0},{1,13},{5,9},{9,5},{13,1},{2,14},{6,10},... | collective-permute-start | bytes 1179656 | tf_op jit(solution)/shard_map/ppermute | solution.py:439
  38.2 11.2 %collective-permute-start.5 = (bf16[512,512]{1,0:T(8,128)(2,1)S(1)}, bf16[512,512]{1,0:T(8,128)(2,1)S(1)}, u32[]{:S(2)}, u32[]{:S(2)}) collective-permute-start(bf16[512,512]{1,0:T(8,128)(2,1)S(1)} %get-tuple-element.42.refs_0_), channel_id=1, source_target_pairs={{4,8},{8,4},{5,9},{9,5},{6,10},{10,6},{7,11},{11,7},{20,24},{24,20... | collective-permute-start | bytes 1572872 | tf_op jit(solution)/shard_map/ppermute | solution.py:445
  38.9 21.0 %collective-permute-start.3 = (bf16[512,512]{1,0:T(8,128)(2,1)S(1)}, bf16[512,512]{1,0:T(8,128)(2,1)S(1)}, u32[]{:S(2)}, u32[]{:S(2)}) collective-permute-start(bf16[512,512]{1,0:T(8,128)(2,1)S(1)} %get-tuple-element.42.refs_0_), channel_id=1, source_target_pairs={{0,4},{4,0},{8,12},{12,8},{1,5},{5,1},{9,13},{13,9},{2,6},{6,2},{1... | collective-permute-start | bytes 1572872 | tf_op jit(solution)/shard_map/ppermute | solution.py:444
  61.7 6.7 %collective-permute-start.7 = (bf16[2,384,512]{2,1,0:T(8,128)(2,1)S(1)}, bf16[2,384,512]{2,1,0:T(8,128)(2,1)S(1)}, u32[]{:S(2)}, u32[]{:S(2)}) collective-permute-start(bf16[2,384,512]{2,1,0:T(8,128)(2,1)S(1)} %get-tuple-element.49), channel_id=1, source_target_pairs={{0,1},{1,0},{2,3},{3,2},{4,5},{5,4},{6,7},{7,6},{8,9},{9,8},{10,11... | collective-permute-start | bytes 2359304 | tf_op jit(solution)/shard_map/ppermute | solution.py:449
  63.5 12.5 %collective-permute-start.9 = (bf16[2,192,768]{2,1,0:T(8,128)(2,1)S(1)}, bf16[2,192,768]{2,1,0:T(8,128)(2,1)S(1)}, u32[]{:S(2)}, u32[]{:S(2)}) collective-permute-start(bf16[2,192,768]{2,1,0:T(8,128)(2,1)S(1)} %get-tuple-element.53), channel_id=1, source_target_pairs={{0,1},{1,0},{2,3},{3,2},{4,5},{5,4},{6,7},{7,6},{8,9},{9,8},{10,11... | collective-permute-start | bytes 1769480 | tf_op jit(solution)/shard_map/ppermute | solution.py:449
  64.0 6.6 %collective-permute-start.6 = (bf16[256,512]{1,0:T(8,128)(2,1)S(1)}, bf16[256,512]{1,0:T(8,128)(2,1)S(1)}, u32[]{:S(2)}, u32[]{:S(2)}) collective-permute-start(bf16[256,512]{1,0:T(8,128)(2,1)S(1)} %get-tuple-element.43.refs_1_), channel_id=1, source_target_pairs={{4,8},{8,4},{5,9},{9,5},{6,10},{10,6},{7,11},{11,7},{20,24},{24,20... | collective-permute-start | bytes 786440 | tf_op jit(solution)/shard_map/ppermute | solution.py:445
  64.9 9.7 %collective-permute-start.4 = (bf16[256,512]{1,0:T(8,128)(2,1)S(1)}, bf16[256,512]{1,0:T(8,128)(2,1)S(1)}, u32[]{:S(2)}, u32[]{:S(2)}) collective-permute-start(bf16[256,512]{1,0:T(8,128)(2,1)S(1)} %get-tuple-element.43.refs_1_), channel_id=1, source_target_pairs={{0,4},{4,0},{8,12},{12,8},{1,5},{5,1},{9,13},{13,9},{2,6},{6,2},{1... | collective-permute-start | bytes 786440 | tf_op jit(solution)/shard_map/ppermute | solution.py:444
  69.1 17.0 %collective-permute-start.8 = (bf16[384,512]{1,0:T(8,128)(2,1)S(1)}, bf16[384,512]{1,0:T(8,128)(2,1)S(1)}, u32[]{:S(2)}, u32[]{:S(2)}) collective-permute-start(bf16[384,512]{1,0:T(8,128)(2,1)S(1)} %get-tuple-element.51), channel_id=1, source_target_pairs={{0,2},{1,3},{2,0},{3,1},{4,6},{5,7},{6,4},{7,5},{8,10},{9,11},{10,... | collective-permute-start | bytes 1179656 | tf_op jit(solution)/shard_map/ppermute | solution.py:451
  75.9 12.8 %collective-permute-start.16 = (bf16[2,384,256]{2,1,0:T(8,128)(2,1)S(1)}, bf16[2,384,256]{2,1,0:T(8,128)(2,1)S(1)}, u32[]{:S(2)}, u32[]{:S(2)}) collective-permute-start(bf16[2,384,256]{2,1,0:T(8,128)(2,1)S(1)} %get-tuple-element.61), channel_id=1, source_target_pairs={{0,1},{1,0},{2,3},{3,2},{4,5},{5,4},{6,7},{7,6},{8,9},{9,8},{10,11... | collective-permute-start | bytes 1179656 | tf_op jit(solution)/shard_map/ppermute | solution.py:449
  76.6 9.5 %collective-permute-start.10 = (bf16[192,768]{1,0:T(8,128)(2,1)S(1)}, bf16[192,768]{1,0:T(8,128)(2,1)S(1)}, u32[]{:S(2)}, u32[]{:S(2)}) collective-permute-start(bf16[192,768]{1,0:T(8,128)(2,1)S(1)} %get-tuple-element.55), channel_id=1, source_target_pairs={{0,2},{1,3},{2,0},{3,1},{4,6},{5,7},{6,4},{7,5},{8,10},{9,11},{10,... | collective-permute-start | bytes 884744 | tf_op jit(solution)/shard_map/ppermute | solution.py:451
  86.8 9.7 %collective-permute-start.11 = (bf16[2,144,512]{2,1,0:T(8,128)(2,1)S(1)}, bf16[2,144,512]{2,1,0:T(8,128)(2,1)S(1)}, u32[]{:S(2)}, u32[]{:S(2)}) collective-permute-start(bf16[2,144,512]{2,1,0:T(8,128)(2,1)S(1)} %get-tuple-element.57), channel_id=1, source_target_pairs={{0,4},{4,0},{8,12},{12,8},{1,5},{5,1},{9,13},{13,9},{2,6},{6,2},{1... | collective-permute-start | bytes 884744 | tf_op jit(solution)/shard_map/ppermute | solution.py:459
  89.3 6.2 %collective-permute-start.17 = (bf16[384,256]{1,0:T(8,128)(2,1)S(1)}, bf16[384,256]{1,0:T(8,128)(2,1)S(1)}, u32[]{:S(2)}, u32[]{:S(2)}) collective-permute-start(bf16[384,256]{1,0:T(8,128)(2,1)S(1)} %get-tuple-element.63), channel_id=1, source_target_pairs={{0,2},{1,3},{2,0},{3,1},{4,6},{5,7},{6,4},{7,5},{8,10},{9,11},{10,... | collective-permute-start | bytes 589832 | tf_op jit(solution)/shard_map/ppermute | solution.py:451
  96.1 6.5 %collective-permute-start.18 = (bf16[2,144,256]{2,1,0:T(8,128)(2,1)S(1)}, bf16[2,144,256]{2,1,0:T(8,128)(2,1)S(1)}, u32[]{:S(2)}, u32[]{:S(2)}) collective-permute-start(bf16[2,144,256]{2,1,0:T(8,128)(2,1)S(1)} %get-tuple-element.65), channel_id=1, source_target_pairs={{0,4},{4,0},{8,12},{12,8},{1,5},{5,1},{9,13},{13,9},{2,6},{6,2},{1... | collective-permute-start | bytes 442376 | tf_op jit(solution)/shard_map/ppermute | solution.py:459
  97.1 9.8 %collective-permute-start.12 = (bf16[144,512]{1,0:T(8,128)(2,1)S(1)}, bf16[144,512]{1,0:T(8,128)(2,1)S(1)}, u32[]{:S(2)}, u32[]{:S(2)}) collective-permute-start(bf16[144,512]{1,0:T(8,128)(2,1)S(1)} %get-tuple-element.59), channel_id=1, source_target_pairs={{0,8},{4,12},{8,0},{12,4},{1,9},{5,13},{9,1},{13,5},{2,10},{6,14},... | collective-permute-start | bytes 442376 | tf_op jit(solution)/shard_map/ppermute | solution.py:461
  103.2 5.9 %collective-permute-start.19 = (bf16[144,256]{1,0:T(8,128)(2,1)S(1)}, bf16[144,256]{1,0:T(8,128)(2,1)S(1)}, u32[]{:S(2)}, u32[]{:S(2)}) collective-permute-start(bf16[144,256]{1,0:T(8,128)(2,1)S(1)} %get-tuple-element.67), channel_id=1, source_target_pairs={{0,8},{4,12},{8,0},{12,4},{1,9},{5,13},{9,1},{13,5},{2,10},{6,14},... | collective-permute-start | bytes 221192 | tf_op jit(solution)/shard_map/ppermute | solution.py:461
  107.5 7.0 %collective-permute-start.13 = (bf16[144,512]{1,0:T(8,128)(2,1)S(1)}, bf16[144,512]{1,0:T(8,128)(2,1)S(1)}, u32[]{:S(2)}, u32[]{:S(2)}) collective-permute-start(bf16[144,512]{1,0:T(8,128)(2,1)S(1)} %shard_map.92.refs_0_), channel_id=1, source_target_pairs={{0,2},{1,3},{2,0},{3,1},{4,6},{5,7},{6,4},{7,5},{8,10},{9,11},{10,... | collective-permute-start | bytes 442376 | tf_op jit(solution)/shard_map/ppermute | solution.py:463
  109.6 4.4 %collective-permute-start.20 = (bf16[144,256]{1,0:T(8,128)(2,1)S(1)}, bf16[144,256]{1,0:T(8,128)(2,1)S(1)}, u32[]{:S(2)}, u32[]{:S(2)}) collective-permute-start(bf16[144,256]{1,0:T(8,128)(2,1)S(1)} %shard_map.97.refs_4_), channel_id=1, source_target_pairs={{0,2},{1,3},{2,0},{3,1},{4,6},{5,7},{6,4},{7,5},{8,10},{9,11},{10,... | collective-permute-start | bytes 221192 | tf_op jit(solution)/shard_map/ppermute | solution.py:463
  110.8 7.7 %collective-permute-start.21 = (bf16[144,256]{1,0:T(8,128)(2,1)S(1)}, bf16[144,256]{1,0:T(8,128)(2,1)S(1)}, u32[]{:S(2)}, u32[]{:S(2)}) collective-permute-start(bf16[144,256]{1,0:T(8,128)(2,1)S(1)} %shard_map.97.refs_4_), channel_id=1, source_target_pairs={{0,1},{1,0},{2,3},{3,2},{4,5},{5,4},{6,7},{7,6},{8,9},{9,8},{10,11... | collective-permute-start | bytes 221192 | tf_op jit(solution)/shard_map/ppermute | solution.py:464
  114.0 4.4 %collective-permute-start.22 = (bf16[144,256]{1,0:T(8,128)(2,1)S(1)}, bf16[144,256]{1,0:T(8,128)(2,1)S(1)}, u32[]{:S(2)}, u32[]{:S(2)}) collective-permute-start(bf16[144,256]{1,0:T(8,128)(2,1)S(1)} %collective-permute-done.20.refs_5_), channel_id=1, source_target_pairs={{0,1},{1,0},{2,3},{3,2},{4,5},{5,4},{6,7},{7,6},{8,9},{9,8},{10,11... | collective-permute-start | bytes 221192 | tf_op jit(solution)/shard_map/ppermute | solution.py:465
  114.0 4.4 %collective-permute-start.14 = (bf16[144,512]{1,0:T(8,128)(2,1)S(1)}, bf16[144,512]{1,0:T(8,128)(2,1)S(1)}, u32[]{:S(2)}, u32[]{:S(2)}) collective-permute-start(bf16[144,512]{1,0:T(8,128)(2,1)S(1)} %shard_map.92.refs_0_), channel_id=1, source_target_pairs={{0,1},{1,0},{2,3},{3,2},{4,5},{5,4},{6,7},{7,6},{8,9},{9,8},{10,11... | collective-permute-start | bytes 442376 | tf_op jit(solution)/shard_map/ppermute | solution.py:464
  114.5 3.9 %collective-permute-start.15 = (bf16[144,512]{1,0:T(8,128)(2,1)S(1)}, bf16[144,512]{1,0:T(8,128)(2,1)S(1)}, u32[]{:S(2)}, u32[]{:S(2)}) collective-permute-start(bf16[144,512]{1,0:T(8,128)(2,1)S(1)} %collective-permute-done.13.refs_1_), channel_id=1, source_target_pairs={{0,1},{1,0},{2,3},{3,2},{4,5},{5,4},{6,7},{7,6},{8,9},{9,8},{10,11... | collective-permute-start | bytes 442376 | tf_op jit(solution)/shard_map/ppermute | solution.py:465
  (4 other events, 22.5 us)
